TPU v7x, 512 devices: a whole 4x8x8 slice. The times are simulated.
512 devices in a mesh: row: 64 (over x, y, core), col: 8 (over z).
Axes of the slice: x: 4, y: 8, z: 8, core: 2. Of those that a mesh axis runs over, the one named last changes fastest.
Arguments:
- panel: float32 [49152, 512], P(('row', 'col')), may hold values from -600 to 600
- trailing: float32 [49152, 4096], P('row', 'col'), may hold values from -6 to 6
Outputs:
- r_factor: float32 [512, 512], replicated
- residual: float32 [49152, 4096], P('row', 'col')
All inputs are finite; a program needn't handle non-finite values.
Results may differ from a plain program's by a relative error of at most 0.0003.
Values sent between devices are 32-bit elements; how exact they have to be, the bound alone decides.
No kernel may reach another device: no remote copies, remote signals or barrier semaphores. Data moves between devices by JAX's collectives and lax.ppermute only.
A program may use at most 64 MiB of HBM per device.

v0:
```python
import functools
import math

import jax
import jax.numpy as jnp
from jax import lax
from jax.experimental import pallas as pl
from jax.experimental.pallas import tpu as pltpu
from jax.sharding import Mesh, PartitionSpec as P


HI = lax.Precision.HIGHEST
B = 512
NB = 128
F32 = jnp.float32


def gram_kernel(which, a_ref, b_ref, out_ref):
    h = B // 2

    def prod(rows, cols):
        total = None
        for ref in (a_ref, b_ref):
            term = lax.dot_general(
                ref[:, rows], ref[:, cols], (((0,), (0,)), ((), ())), precision=HI, preferred_element_type=F32
            )
            total = term if total is None else total + term
        return total

    def put(j, v):
        for i in range(v.shape[1] // NB):
            out_ref[:, j + i, :] = v[:, i * NB:(i + 1) * NB]

    @pl.when(which[0] == 0)
    def _():
        put(0, prod(slice(0, h), slice(0, 384)))

    @pl.when(which[0] != 0)
    def _():
        put(0, prod(slice(0, h), slice(384, B)))
        put(1, prod(slice(h, B), slice(h, B)))


def sub_row(v, j):
    return jnp.broadcast_to(v[j:j + 1, :], v.shape)


def factor_block(get, put_r, put_inv):
    sub = lax.broadcasted_iota(jnp.int32, (8, NB), 0)
    lane = lax.broadcasted_iota(jnp.int32, (8, NB), 1)
    a = [get(t) for t in range(NB // 8)]
    y = [jnp.where(lane == sub + 8 * t, 1.0, 0.0).astype(jnp.float32) for t in range(NB // 8)]
    for s in range(NB // 8):
        k = 8 * s
        av, yv = a[s], y[s]
        cols = [jnp.broadcast_to(av[:, k + j:k + j + 1], (8, NB)) for j in range(8)]
        rows_r = jnp.zeros((8, NB), jnp.float32)
        rows_y = jnp.zeros((8, NB), jnp.float32)
        for j in range(8):
            here = sub == j
            d = sub_row(cols[j], j)
            rs = lax.rsqrt(d)
            inv = rs * rs
            ra, ry = sub_row(av, j), sub_row(yv, j)
            rows_r = jnp.where(here, ra * rs, rows_r)
            rows_y = jnp.where(here, ry * rs, rows_y)
            av = jnp.where(here, ra * inv, av - (cols[j] * ra) * inv)
            yv = jnp.where(here, ry * inv, yv - (cols[j] * ry) * inv)
            for m in range(j + 1, 8):
                cm = sub_row(cols[m], j)
                cols[m] = jnp.where(here, cm * inv, cols[m] - (cols[j] * cm) * inv)
        put_r(s, rows_r)
        put_inv(s, rows_y)
        va = [sub_row(av, j) for j in range(8)]
        vy = [sub_row(yv, j) for j in range(8)]
        for t in range(s + 1, NB // 8):
            at, yt = a[t], y[t]
            lc = [jnp.broadcast_to(at[:, k + j:k + j + 1], (8, NB)) for j in range(8)]
            pa = [lc[j] * va[j] for j in range(8)]
            py = [lc[j] * vy[j] for j in range(8)]
            tree = lambda p: ((p[0] + p[1]) + (p[2] + p[3])) + ((p[4] + p[5]) + (p[6] + p[7]))
            a[t] = at - tree(pa)
            y[t] = yt - tree(py)


def run_block(aug, inv, at, width, blocks, r_ref, m_ref, scale, a_from):
    b = at // NB

    def get(t):
        return aug[pl.ds(pl.multiple_of(at + 8 * t, 8), 8), pl.ds(at, NB)]

    def put_inv(s, v):
        inv[8 * s:8 * s + 8, :] = v

    def put_r(s, v):
        inv[NB + 8 * s:NB + 8 * s + 8, :] = v

    factor_block(get, put_r, put_inv)
    rows = jnp.dot(inv[0:NB, :], aug[pl.ds(at, NB), :], precision=HI, preferred_element_type=F32)
    aug[pl.ds(at, NB), :] = rows
    row = lax.broadcasted_iota(jnp.int32, (NB, width), 0)
    col = lax.broadcasted_iota(jnp.int32, (NB, width), 1)
    m_ref(at, rows[:, width:])
    r_ref(at, jnp.where(col > row + at, rows[:, :width], 0.0) * scale)
    r2 = lax.broadcasted_iota(jnp.int32, (NB, NB), 0)
    c2 = lax.broadcasted_iota(jnp.int32, (NB, NB), 1)
    a_from(at, jnp.where(c2 >= r2, inv[NB:2 * NB, :], 0.0) * scale)
    for i in range(1, blocks):
        @pl.when(i > b)
        def _():
            left = aug[pl.ds(at, NB), i * NB:(i + 1) * NB]
            upd = lax.dot_general(
                left, aug[pl.ds(at, NB), :], (((0,), (0,)), ((), ())), precision=HI, preferred_element_type=F32
            )
            aug[i * NB:(i + 1) * NB, :] -= upd


def top_kernel(scale, which, mine_ref, other_ref, r_out, m_out, tail_out, aug, inv):
    h = B // 2

    def load(lo, hi):
        for i in range(3):
            aug[0:h, i * NB:(i + 1) * NB] = lo[:, i, :]
        aug[0:h, 384:B] = hi[:, 0, :]
        for i in range(2):
            aug[h:B, h + i * NB:h + (i + 1) * NB] = hi[:, 1 + i, :]

    @pl.when(which[0] == 0)
    def _():
        load(mine_ref, other_ref)

    @pl.when(which[0] != 0)
    def _():
        load(other_ref, mine_ref)

    aug[h:B, 0:h] = jnp.zeros((h, h), F32)
    ri = lax.broadcasted_iota(jnp.int32, (h, h), 0)
    ci = lax.broadcasted_iota(jnp.int32, (h, h), 1)
    aug[0:h, B:] = jnp.where(ri == ci, 1.0, 0.0).astype(F32)
    aug[h:B, B:] = jnp.zeros((h, h), F32)

    def block(b, _):
        at = pl.multiple_of(b * NB, NB)

        def put_m(at, v):
            m_out[pl.ds(at, NB), :] = v

        def put_r(at, v):
            r_out[pl.ds(at, NB), :] = v

        def put_d(at, v):
            r_out[pl.ds(at, NB), pl.ds(at, NB)] = v

        run_block(aug, inv, at, B, B // NB, put_r, put_m, scale, put_d)
        return 0

    lax.fori_loop(0, 2, block, 0)
    tail_out[...] = aug[h:B, h:]


def low_kernel(scale, top_ref, mtop_ref, tail_ref, r_out, m_out, aug, inv):
    h = B // 2
    r_out[0:h, :] = top_ref[...]
    r_out[h:B, 0:h] = jnp.zeros((h, h), F32)
    m_out[0:h, 0:h] = mtop_ref[...]
    m_out[0:h, h:B] = jnp.zeros((h, h), F32)
    aug[:, 0:B] = tail_ref[...]
    ri = lax.broadcasted_iota(jnp.int32, (h, h), 0)
    ci = lax.broadcasted_iota(jnp.int32, (h, h), 1)
    aug[:, B:] = jnp.where(ri == ci, 1.0, 0.0).astype(F32)

    def block(b, _):
        at = pl.multiple_of(b * NB, NB)

        def put_m(at, v):
            m_out[pl.ds(at + h, NB), :] = v

        def put_r(at, v):
            r_out[pl.ds(at + h, NB), h:B] = v

        def put_d(at, v):
            r_out[pl.ds(at + h, NB), pl.ds(at + h, NB)] = v

        run_block(aug, inv, at, h, 2, put_r, put_m, scale, put_d)
        return 0

    lax.fori_loop(0, 2, block, 0)


VM = pl.BlockSpec(memory_space=pltpu.VMEM)
SM = pl.BlockSpec(memory_space=pltpu.SMEM)


def gram(which, panel, partner):
    return pl.pallas_call(
        gram_kernel,
        out_shape=jax.ShapeDtypeStruct((B // 2, 3, NB), F32),
        in_specs=[SM, VM, VM],
        out_specs=VM,
        name="gram",
    )(which, panel, partner)


def factor_top(which, mine, other, total_rows):
    h = B // 2
    return pl.pallas_call(
        functools.partial(top_kernel, 1.0 / math.sqrt(total_rows)),
        out_shape=[jax.ShapeDtypeStruct(s, F32) for s in ((h, B), (h, h), (h, B))],
        in_specs=[SM, VM, VM],
        out_specs=[VM] * 3,
        scratch_shapes=[pltpu.VMEM((B, B + h), F32), pltpu.VMEM((2 * NB, NB), F32)],
        name="factor_top",
    )(which, mine, other)


def factor_low(top, top_inverse, tail, total_rows):
    h = B // 2
    return pl.pallas_call(
        functools.partial(low_kernel, 1.0 / math.sqrt(total_rows)),
        out_shape=[jax.ShapeDtypeStruct((B, B), F32)] * 2,
        in_specs=[VM] * 3,
        out_specs=[VM] * 2,
        scratch_shapes=[pltpu.VMEM((h, h + B), F32), pltpu.VMEM((2 * NB, NB), F32)],
        name="factor_low",
    )(top, top_inverse, tail)


def dot(a, b, dims, precision=HI):
    return lax.dot_general(a, b, (dims, ((), ())), precision=precision, preferred_element_type=jnp.float32)


def spread(own, axes, parts):
    copies = jnp.broadcast_to(own[None], (parts,) + own.shape)
    return lax.all_to_all(copies, axes, 0, 0, tiled=True)


def per_device(panel, trailing):
    high = lax.Precision.HIGH
    axes, plane = ("x", "y", "z"), ("x", "y")
    everyone, ring, depth = lax.axis_size(axes), lax.axis_size(plane), lax.axis_size("z")
    total_rows = panel.shape[0] * everyone * 2
    core = lax.axis_index("c")
    place = lax.axis_index("z")
    swap = [(0, 1), (1, 0)]
    h = B // 2
    each = panel.shape[0]
    which = jnp.full((1,), core, jnp.int32)

    block = jnp.zeros((depth * each, B), jnp.float32)
    block = lax.dynamic_update_slice(block, panel, (place * each, 0))
    forth = back = panel
    for k in range(1, depth // 2 + 1):
        forth = lax.ppermute(forth, "z", [(i, (i + 1) % depth) for i in range(depth)])
        block = lax.dynamic_update_slice(block, forth, ((place + depth - k) % depth * each, 0))
        if k < depth - k:
            back = lax.ppermute(back, "z", [(i, (i - 1) % depth) for i in range(depth)])
            block = lax.dynamic_update_slice(block, back, ((place + k) % depth * each, 0))

    partner = lax.ppermute(panel, "c", swap)
    half = gram(which, panel, partner)
    pieces = lax.all_to_all(half.reshape((everyone, -1) + half.shape[2:]) if everyone != h else half, axes, 0, 0, tiled=True)
    own = jnp.sum(pieces, axis=0)
    mine = spread(own, axes, everyone).reshape(half.shape)
    other = lax.ppermute(mine, "c", swap)
    top, top_inverse, tail = factor_top(which, mine, other, total_rows)
    upper, inverse = factor_low(top, top_inverse, tail, total_rows)

    give = dot(lax.dynamic_slice(block, (0, (1 - core) * h), (depth * each, h)), trailing, ((0,), (0,)), high)
    got = lax.ppermute(give, "c", swap)
    keep = dot(lax.dynamic_slice(block, (0, core * h), (depth * each, h)), trailing, ((0,), (0,)), high)
    pieces = lax.all_to_all((keep + got).reshape(ring, h // ring, -1), plane, 0, 0, tiled=True)
    own = jnp.sum(pieces, axis=0)
    near = spread(own, plane, ring).reshape(h, -1)
    far = lax.ppermute(near, "c", swap)

    ginv = dot(inverse, inverse, ((0,), (0,)))
    weights = dot(lax.dynamic_slice(ginv, (core * h, 0), (h, B)), near, ((0,), (0,)))
    weights = weights + dot(lax.dynamic_slice(ginv, ((1 - core) * h, 0), (h, B)), far, ((0,), (0,)))
    residual = trailing - dot(block, weights, ((1,), (0,)), high)
    return (upper, residual)


def solution(mesh):
    row, col = mesh.devices.shape
    y = 8 if row == 64 else 2
    fine = Mesh(mesh.devices.reshape(row // (2 * y), y, 2, col), ("x", "y", "c", "z"))
    row_axes = ("x", "y", "c")
    return jax.shard_map(
        per_device,
        mesh=fine,
        in_specs=(P(row_axes + ("z",), None), P(row_axes, "z")),
        out_specs=(P(), P(row_axes, "z")),
        check_vma=False,
    )
```

profile of v0, /device:TPU:1, one launch (start us, length us, event | category | flops | bytes accessed | tf_op | source)
XLA Modules:
  0.0 192.5 jit_solution(4613638203009459231)
XLA Ops:
  0.6 0.0 copy-start.1
  0.6 8.9 %collective-permute-start = (f32[96,512]{1,0:T(8,128)}, f32[96,512]{1,0:T(8,128)S(1)}, u32[]{:S(2)}, u32[]{:S(2)}) collective-permute-start(f32[96,512]{1,0:T(8,128)} %a_ref.1), channel_id=1, source_target_pairs={{0,8},{8,0},{1,9},{9,1},{2,10},{10,2},{3,11},{11,3},{4,12},{12,4},... | collective-permute-start | bytes 589832 | tf_op jit(solution)/shard_map/ppermute | solution.py:259
  9.5 1.9 collective-permute-start.2
  11.5 5.3 %collective-permute-start.3 = (f32[96,512]{1,0:T(8,128)}, f32[96,512]{1,0:T(8,128)S(1)}, u32[]{:S(2)}, u32[]{:S(2)}) collective-permute-start(f32[96,512]{1,0:T(8,128)} %a_ref.1), channel_id=1, source_target_pairs={{0,7},{1,0},{2,1},{3,2},{4,3},{5,4},{6,5},{7,6},{8,15},{9,8},{10,9... | collective-permute-start | bytes 589832 | tf_op jit(solution)/shard_map/ppermute | solution.py:256
  16.9 0.2 broadcast_in_dim.20
  17.1 0.0 collective-permute-done.b_ref
  17.2 0.0 copy-start.2
  17.2 0.7 copy-done.2
  17.8 2.8 %gram.1 = f32[256,3,128]{2,1,0:T(4,128)} custom-call(s32[1]{0:T(128)} %bitcast.which, f32[96,512]{1,0:T(8,128)} %a_ref.1, f32[96,512]{1,0:T(8,128)} %copy-done.2), custom_call_target="tpu_custom_call" | custom-call | tf_op jit(solution)/shard_map/gram/pallas_call | solution.py:195
  20.6 17.3 %all-to-all-start = ((f32[256,3,128]{2,1,0:T(4,128)}), f32[256,3,128]{2,1,0:T(4,128)}, u32[]{:S(2)}, u32[]{:S(2)}) async-start(f32[256,3,128]{2,1,0:T(4,128)} %gram.1), calls=%async_computation | async-start | bytes 1048576 | tf_op jit(solution)/shard_map/all_to_all | solution.py:261
  37.9 0.0 copy-start
  37.9 0.0 collective-permute-done.2
  37.9 2.1 %collective-permute-start.4 = (f32[96,512]{1,0:T(8,128)}, f32[96,512]{1,0:T(8,128)S(1)}, u32[]{:S(2)}, u32[]{:S(2)}) collective-permute-start(f32[96,512]{1,0:T(8,128)} %collective-permute-done.2), channel_id=1, source_target_pairs={{0,1},{1,2},{2,3},{3,4},{4,5},{5,6},{6,7},{7,0},{8,9},{9,10},{10,1... | collective-permute-start | bytes 589832 | tf_op jit(solution)/shard_map/ppermute | solution.py:253
  40.0 0.0 collective-permute-done.3
  40.0 4.6 %collective-permute-start.5 = (f32[96,512]{1,0:T(8,128)S(1)}, f32[96,512]{1,0:T(8,128)S(1)}, u32[]{:S(2)}, u32[]{:S(2)}) collective-permute-start(f32[96,512]{1,0:T(8,128)S(1)} %collective-permute-done.3), channel_id=1, source_target_pairs={{0,7},{1,0},{2,1},{3,2},{4,3},{5,4},{6,5},{7,6},{8,15},{9,8},{10,9... | collective-permute-start | bytes 589832 | tf_op jit(solution)/shard_map/ppermute | solution.py:256
  44.6 0.9 constant_dynamic-update-slice_fusion.6
  45.6 9.3 %collective-permute-done.4 = f32[96,512]{1,0:T(8,128)S(1)} collective-permute-done((f32[96,512]{1,0:T(8,128)}, f32[96,512]{1,0:T(8,128)S(1)}, u32[]{:S(2)}, u32[]{:S(2)}) %collective-permute-start.4) | collective-permute-done | bytes 196640 | tf_op jit(solution)/shard_map/ppermute | solution.py:253
  54.9 1.9 collective-permute-start.6
  56.8 0.0 collective-permute-done.5
  56.8 4.6 %collective-permute-start.7 = (f32[96,512]{1,0:T(8,128)S(1)}, f32[96,512]{1,0:T(8,128)S(1)}, u32[]{:S(2)}, u32[]{:S(2)}) collective-permute-start(f32[96,512]{1,0:T(8,128)S(1)} %collective-permute-done.5), channel_id=1, source_target_pairs={{0,7},{1,0},{2,1},{3,2},{4,3},{5,4},{6,5},{7,6},{8,15},{9,8},{10,9... | collective-permute-start | bytes 589832 | tf_op jit(solution)/shard_map/ppermute | solution.py:256
  61.4 2.5 %collective-permute-done.6 = f32[96,512]{1,0:T(8,128)S(1)} collective-permute-done((f32[96,512]{1,0:T(8,128)S(1)}, f32[96,512]{1,0:T(8,128)S(1)}, u32[]{:S(2)}, u32[]{:S(2)}) %collective-permute-start.6) | collective-permute-done | bytes 196640 | tf_op jit(solution)/shard_map/ppermute | solution.py:253
  64.0 1.9 collective-permute-start.8
  66.0 6.3 %collective-permute-done.8 = f32[96,512]{1,0:T(8,128)S(1)} collective-permute-done((f32[96,512]{1,0:T(8,128)S(1)}, f32[96,512]{1,0:T(8,128)S(1)}, u32[]{:S(2)}, u32[]{:S(2)}) %collective-permute-start.8) | collective-permute-done | bytes 196640 | tf_op jit(solution)/shard_map/ppermute | solution.py:253
  72.3 1.6 fusion.1
  73.9 4.1 %collective-permute-start.9 = (f32[256,512]{1,0:T(8,128)}, f32[256,512]{1,0:T(8,128)}, u32[]{:S(2)}, u32[]{:S(2)}) collective-permute-start(f32[256,512]{1,0:T(8,128)} %fusion.1), channel_id=1, source_target_pairs={{0,8},{8,0},{1,9},{9,1},{2,10},{10,2},{3,11},{11,3},{4,12},{12,4},... | collective-permute-start | bytes 1572872 | tf_op jit(solution)/shard_map/ppermute | solution.py:269
  78.0 1.9 collective-permute-done.9
  79.9 2.7 %fusion = f32[32,8,512]{2,1,0:T(8,128)} fusion(f32[256,512]{1,0:T(8,128)} %collective-permute-done.9, f32[768,512]{1,0:T(8,128)S(1)} %copy-done, f32[768,512]{1,0:T(8,128)S(1)} %constant_dynamic-update-slice_fusion, s32[]{:T(128)S(6)} %select_n.78), kind=kOutput, calls=%fused_computation.3 | convolution fusion | flops 604110848 | bytes 3407876 | tf_op jit(solution)/shard_map/dot_general | solution.py:229
  82.6 0.0 all-to-all-done
  82.6 8.7 %all-to-all-start.2 = ((f32[32,8,512]{2,1,0:T(8,128)}), f32[32,8,512]{2,1,0:T(8,128)}, u32[]{:S(2)}, u32[]{:S(2)}) async-start(f32[32,8,512]{2,1,0:T(8,128)} %fusion), calls=%async_computation.2 | async-start | bytes 1048576 | tf_op jit(solution)/shard_map/all_to_all | solution.py:271
  91.4 1.3 reduce_sum.18
  92.7 12.7 %all-to-all-done.2 = f32[32,8,512]{2,1,0:T(8,128)} async-done(((f32[32,8,512]{2,1,0:T(8,128)}), f32[32,8,512]{2,1,0:T(8,128)}, u32[]{:S(2)}, u32[]{:S(2)}) %all-to-all-start.2) | async-done | bytes 524320 | tf_op jit(solution)/shard_map/all_to_all | solution.py:271
  105.4 0.9 broadcast_in_dim.9
  106.3 15.5 %all-to-all-start.1 = ((f32[256,3,128]{2,1,0:T(4,128)}), f32[256,3,128]{2,1,0:T(4,128)}, u32[]{:S(2)}, u32[]{:S(2)}) async-start(f32[256,3,128]{2,1,0:T(4,128)} %broadcast_in_dim.9), calls=%async_computation.1 | async-start | bytes 1048576 | tf_op jit(solution)/shard_map/all_to_all | solution.py:234
  121.8 1.1 reduce_sum.19
  122.9 15.8 %all-to-all-done.1.mine_ref = f32[256,3,128]{2,1,0:T(4,128)} async-done(((f32[256,3,128]{2,1,0:T(4,128)}), f32[256,3,128]{2,1,0:T(4,128)}, u32[]{:S(2)}, u32[]{:S(2)}) %all-to-all-start.1) | async-done | bytes 393248 | tf_op jit(solution)/shard_map/all_to_all | solution.py:234
  138.7 0.9 broadcast_in_dim.21
  139.6 6.1 %all-to-all-start.3 = ((f32[32,8,512]{2,1,0:T(8,128)}), f32[32,8,512]{2,1,0:T(8,128)}, u32[]{:S(2)}, u32[]{:S(2)}) async-start(f32[32,8,512]{2,1,0:T(8,128)} %broadcast_in_dim.21), calls=%async_computation.3 | async-start | bytes 1048576 | tf_op jit(solution)/shard_map/all_to_all | solution.py:234
  145.7 3.8 %collective-permute-start.1 = (f32[256,3,128]{2,1,0:T(4,128)}, f32[256,3,128]{2,1,0:T(4,128)}, u32[]{:S(2)}, u32[]{:S(2)}) collective-permute-start(f32[256,3,128]{2,1,0:T(4,128)} %all-to-all-done.1.mine_ref), channel_id=1, source_target_pairs={{0,8},{8,0},{1,9},{9,1},{2,10},{10,2},{3,11},{11,3},{4,12},{12,4},... | collective-permute-start | bytes 1179656 | tf_op jit(solution)/shard_map/ppermute | solution.py:264
  149.5 1.9 collective-permute-done.1.other_ref
  151.4 15.7 %factor_top.1 = (f32[256,512]{1,0:T(8,128)}, f32[256,256]{1,0:T(8,128)}, f32[256,512]{1,0:T(8,128)}) custom-call(s32[1]{0:T(128)} %bitcast.which, f32[256,3,128]{2,1,0:T(4,128)} %all-to-all-done.1.mine_ref, f32[256,3,128]{2,1,0:T(4,128)} %collective-permute-done.1.other_ref), custom_call_target="tpu_custom_call" | custom-call | tf_op jit(solution)/shard_map/factor_top/pallas_call | solution.py:206
  167.1 13.7 %factor_low.1 = (f32[512,512]{1,0:T(8,128)}, f32[512,512]{1,0:T(8,128)}) custom-call(f32[256,512]{1,0:T(8,128)} %get-tuple-element.7.top_ref, f32[256,256]{1,0:T(8,128)} %get-tuple-element.8.mtop_ref, f32[256,512]{1,0:T(8,128)} %get-tuple-element.9.tail_ref), custom_call_target="tpu_custom_call" | custom-call | tf_op jit(solution)/shard_map/factor_low/pallas_call | solution.py:218
  180.8 0.0 all-to-all-done.3
  180.8 2.5 %collective-permute-start.10 = (f32[256,512]{1,0:T(8,128)}, f32[256,512]{1,0:T(8,128)S(1)}, u32[]{:S(2)}, u32[]{:S(2)}) collective-permute-start(f32[256,512]{1,0:T(8,128)} %bitcast.2), channel_id=1, source_target_pairs={{0,8},{8,0},{1,9},{9,1},{2,10},{10,2},{3,11},{11,3},{4,12},{12,4},... | collective-permute-start | bytes 1572872 | tf_op jit(solution)/shard_map/ppermute | solution.py:274
  183.2 3.5 %fusion.12 = f32[512,512]{1,0:T(8,128)S(1)} fusion(f32[512,512]{1,0:T(8,128)} %get-tuple-element.11), kind=kOutput, calls=%fused_computation.23 | convolution fusion | flops 1610612736 | bytes 2097152 | tf_op jit(solution)/shard_map/dot_general | solution.py:229
  186.7 2.1 %fusion.5 = f32[512,512]{1,0:T(8,128)S(1)} fusion(f32[512,512]{1,0:T(8,128)S(1)} %fusion.12, s32[]{:T(128)S(6)} %select_n.78, f32[32,8,512]{2,1,0:T(8,128)} %all-to-all-done.3), kind=kOutput, calls=%fused_computation.8 | convolution fusion | flops 805306368 | bytes 2097156 | tf_op jit(solution)/shard_map/dot_general | solution.py:229
  188.8 0.0 collective-permute-done.10
  188.8 1.1 convolution_add_fusion
  189.9 2.6 %convolution_subtract_fusion = f32[768,512]{1,0:T(8,128)} fusion(f32[768,512]{1,0:T(8,128)S(1)} %copy-done, f32[768,512]{1,0:T(8,128)S(1)} %constant_dynamic-update-slice_fusion, f32[512,512]{1,0:T(8,128)S(1)} %convolution_add_fusion), kind=kOutput, calls=%fused_computation | convolution fusion | flops 1208352768 | bytes 5767168 | tf_op jit(solution)/shard_map/dot_general | solution.py:229
  (10 shorter events, 0.1 us)
Async XLA Ops:
  0.6 16.5 %copy-start.1 = (f32[96,512]{1,0:T(8,128)S(1)}, f32[96,512]{1,0:T(8,128)}, u32[]{:S(2)}) copy-start(f32[96,512]{1,0:T(8,128)} %a_ref.1) | copy-start | bytes 589828
  0.6 16.5 %collective-permute-start = (f32[96,512]{1,0:T(8,128)}, f32[96,512]{1,0:T(8,128)S(1)}, u32[]{:S(2)}, u32[]{:S(2)}) collective-permute-start(f32[96,512]{1,0:T(8,128)} %a_ref.1), channel_id=1, source_target_pairs={{0,8},{8,0},{1,9},{9,1},{2,10},{10,2},{3,11},{11,3},{4,12},{12,4},... | collective-permute-start | bytes 589832 | tf_op jit(solution)/shard_map/ppermute | solution.py:259
  9.5 28.4 %collective-permute-start.2 = (f32[96,512]{1,0:T(8,128)}, f32[96,512]{1,0:T(8,128)}, u32[]{:S(2)}, u32[]{:S(2)}) collective-permute-start(f32[96,512]{1,0:T(8,128)} %a_ref.1), channel_id=1, source_target_pairs={{0,1},{1,2},{2,3},{3,4},{4,5},{5,6},{6,7},{7,0},{8,9},{9,10},{10,1... | collective-permute-start | bytes 589832 | tf_op jit(solution)/shard_map/ppermute | solution.py:253
  11.5 28.5 %collective-permute-start.3 = (f32[96,512]{1,0:T(8,128)}, f32[96,512]{1,0:T(8,128)S(1)}, u32[]{:S(2)}, u32[]{:S(2)}) collective-permute-start(f32[96,512]{1,0:T(8,128)} %a_ref.1), channel_id=1, source_target_pairs={{0,7},{1,0},{2,1},{3,2},{4,3},{5,4},{6,5},{7,6},{8,15},{9,8},{10,9... | collective-permute-start | bytes 589832 | tf_op jit(solution)/shard_map/ppermute | solution.py:256
  17.2 0.7 copy-start.2
  20.6 62.0 %all-to-all-start = ((f32[256,3,128]{2,1,0:T(4,128)}), f32[256,3,128]{2,1,0:T(4,128)}, u32[]{:S(2)}, u32[]{:S(2)}) async-start(f32[256,3,128]{2,1,0:T(4,128)} %gram.1), calls=%async_computation | async-start | bytes 1048576 | tf_op jit(solution)/shard_map/all_to_all | solution.py:261
  37.9 34.3 %copy-start = (f32[768,512]{1,0:T(8,128)S(1)}, f32[768,512]{1,0:T(8,128)}, u32[]{:S(2)}) copy-start(f32[768,512]{1,0:T(8,128)} %param.3) | copy-start | bytes 4718596
  37.9 16.9 %collective-permute-start.4 = (f32[96,512]{1,0:T(8,128)}, f32[96,512]{1,0:T(8,128)S(1)}, u32[]{:S(2)}, u32[]{:S(2)}) collective-permute-start(f32[96,512]{1,0:T(8,128)} %collective-permute-done.2), channel_id=1, source_target_pairs={{0,1},{1,2},{2,3},{3,4},{4,5},{5,6},{6,7},{7,0},{8,9},{9,10},{10,1... | collective-permute-start | bytes 589832 | tf_op jit(solution)/shard_map/ppermute | solution.py:253
  40.0 16.8 %collective-permute-start.5 = (f32[96,512]{1,0:T(8,128)S(1)}, f32[96,512]{1,0:T(8,128)S(1)}, u32[]{:S(2)}, u32[]{:S(2)}) collective-permute-start(f32[96,512]{1,0:T(8,128)S(1)} %collective-permute-done.3), channel_id=1, source_target_pairs={{0,7},{1,0},{2,1},{3,2},{4,3},{5,4},{6,5},{7,6},{8,15},{9,8},{10,9... | collective-permute-start | bytes 589832 | tf_op jit(solution)/shard_map/ppermute | solution.py:256
  54.9 9.1 %collective-permute-start.6 = (f32[96,512]{1,0:T(8,128)S(1)}, f32[96,512]{1,0:T(8,128)S(1)}, u32[]{:S(2)}, u32[]{:S(2)}) collective-permute-start(f32[96,512]{1,0:T(8,128)S(1)} %collective-permute-done.4), channel_id=1, source_target_pairs={{0,1},{1,2},{2,3},{3,4},{4,5},{5,6},{6,7},{7,0},{8,9},{9,10},{10,1... | collective-permute-start | bytes 589832 | tf_op jit(solution)/shard_map/ppermute | solution.py:253
  56.8 9.1 %collective-permute-start.7 = (f32[96,512]{1,0:T(8,128)S(1)}, f32[96,512]{1,0:T(8,128)S(1)}, u32[]{:S(2)}, u32[]{:S(2)}) collective-permute-start(f32[96,512]{1,0:T(8,128)S(1)} %collective-permute-done.5), channel_id=1, source_target_pairs={{0,7},{1,0},{2,1},{3,2},{4,3},{5,4},{6,5},{7,6},{8,15},{9,8},{10,9... | collective-permute-start | bytes 589832 | tf_op jit(solution)/shard_map/ppermute | solution.py:256
  64.0 8.3 %collective-permute-start.8 = (f32[96,512]{1,0:T(8,128)S(1)}, f32[96,512]{1,0:T(8,128)S(1)}, u32[]{:S(2)}, u32[]{:S(2)}) collective-permute-start(f32[96,512]{1,0:T(8,128)S(1)} %collective-permute-done.6), channel_id=1, source_target_pairs={{0,1},{1,2},{2,3},{3,4},{4,5},{5,6},{6,7},{7,0},{8,9},{9,10},{10,1... | collective-permute-start | bytes 589832 | tf_op jit(solution)/shard_map/ppermute | solution.py:253
  73.9 6.0 %collective-permute-start.9 = (f32[256,512]{1,0:T(8,128)}, f32[256,512]{1,0:T(8,128)}, u32[]{:S(2)}, u32[]{:S(2)}) collective-permute-start(f32[256,512]{1,0:T(8,128)} %fusion.1), channel_id=1, source_target_pairs={{0,8},{8,0},{1,9},{9,1},{2,10},{10,2},{3,11},{11,3},{4,12},{12,4},... | collective-permute-start | bytes 1572872 | tf_op jit(solution)/shard_map/ppermute | solution.py:269
  82.6 22.8 %all-to-all-start.2 = ((f32[32,8,512]{2,1,0:T(8,128)}), f32[32,8,512]{2,1,0:T(8,128)}, u32[]{:S(2)}, u32[]{:S(2)}) async-start(f32[32,8,512]{2,1,0:T(8,128)} %fusion), calls=%async_computation.2 | async-start | bytes 1048576 | tf_op jit(solution)/shard_map/all_to_all | solution.py:271
  106.3 32.5 %all-to-all-start.1 = ((f32[256,3,128]{2,1,0:T(4,128)}), f32[256,3,128]{2,1,0:T(4,128)}, u32[]{:S(2)}, u32[]{:S(2)}) async-start(f32[256,3,128]{2,1,0:T(4,128)} %broadcast_in_dim.9), calls=%async_computation.1 | async-start | bytes 1048576 | tf_op jit(solution)/shard_map/all_to_all | solution.py:234
  139.6 41.2 %all-to-all-start.3 = ((f32[32,8,512]{2,1,0:T(8,128)}), f32[32,8,512]{2,1,0:T(8,128)}, u32[]{:S(2)}, u32[]{:S(2)}) async-start(f32[32,8,512]{2,1,0:T(8,128)} %broadcast_in_dim.21), calls=%async_computation.3 | async-start | bytes 1048576 | tf_op jit(solution)/shard_map/all_to_all | solution.py:234
  145.7 5.7 %collective-permute-start.1 = (f32[256,3,128]{2,1,0:T(4,128)}, f32[256,3,128]{2,1,0:T(4,128)}, u32[]{:S(2)}, u32[]{:S(2)}) collective-permute-start(f32[256,3,128]{2,1,0:T(4,128)} %all-to-all-done.1.mine_ref), channel_id=1, source_target_pairs={{0,8},{8,0},{1,9},{9,1},{2,10},{10,2},{3,11},{11,3},{4,12},{12,4},... | collective-permute-start | bytes 1179656 | tf_op jit(solution)/shard_map/ppermute | solution.py:264
  180.8 8.1 %collective-permute-start.10 = (f32[256,512]{1,0:T(8,128)}, f32[256,512]{1,0:T(8,128)S(1)}, u32[]{:S(2)}, u32[]{:S(2)}) collective-permute-start(f32[256,512]{1,0:T(8,128)} %bitcast.2), channel_id=1, source_target_pairs={{0,8},{8,0},{1,9},{9,1},{2,10},{10,2},{3,11},{11,3},{4,12},{12,4},... | collective-permute-start | bytes 1572872 | tf_op jit(solution)/shard_map/ppermute | solution.py:274
where the time goes:
time: 194 us; the launch traced here: 192 us
  starting transfers between devices  89.3 us (46%)
  waiting for transfers between devices  50.4 us (26%)
  Pallas kernels  32.1 us (17%)
  matrix products  13.6 us (7%)
  local copies, waits for them, and re-layouts  3.68 us (2%)
  other arithmetic  2.41 us (1%)
    all_to_all x2, starting transfers between devices, spread(): return lax.all_to_all(copies, axes, 0, 0, tiled=True)  21.6 us
    ppermute x4, waiting for transfers between devices, per_device(): lax.ppermute(forth, 'z', [(i, (i + 1) % depth) for i in range(depth)])  18.1 us
    all_to_all x1, starting transfers between devices, per_device(): lax.all_to_all(half.reshape((everyone, -1) + half.shape[2:]) if everyone...  17.3 us
    all_to_all x2, waiting for transfers between devices, spread(): return lax.all_to_all(copies, axes, 0, 0, tiled=True)  15.8 us
    pallas_call x1, Pallas kernels, factor_top(): pl.pallas_call(functools.partial(top_kernel, 1.0 / math.sqrt(total_rows))...  15.7 us
    ppermute x3, starting transfers between devices, per_device(): back = lax.ppermute(back, 'z', [(i, (i - 1) % depth) for i in range(depth)])  14.5 us
    pallas_call x1, Pallas kernels, factor_low(): pl.pallas_call(functools.partial(low_kernel, 1.0 / math.sqrt(total_rows))...  13.7 us
    dot_general x6, matrix products, dot(): lax.dot_general(a, b, (dims, ((), ())), precision=precision, preferred_el...  13.6 us
  transfers between devices with their start and end apart: 15, of which 7 were waited for; matrix products, arithmetic and copies ran while one was open for 7% of the time, Pallas kernels for 17%

commit v1 on v0

--- a/solution.py
+++ b/solution.py
@@ -29,7 +29,8 @@
 
     def put(j, v):
         for i in range(v.shape[1] // NB):
-            out_ref[:, j + i, :] = v[:, i * NB:(i + 1) * NB]
+            tiles = v[:, i * NB:(i + 1) * NB].reshape(h // 8, 8, NB)
+            out_ref[:, 8 * (j + i):8 * (j + i + 1), :] = tiles
 
     @pl.when(which[0] == 0)
     def _():
@@ -119,11 +120,14 @@
     h = B // 2
 
     def load(lo, hi):
+        def tiles(ref, i):
+            return ref[:, 8 * i:8 * i + 8, :].reshape(h, NB)
+
         for i in range(3):
-            aug[0:h, i * NB:(i + 1) * NB] = lo[:, i, :]
-        aug[0:h, 384:B] = hi[:, 0, :]
+            aug[0:h, i * NB:(i + 1) * NB] = tiles(lo, i)
+        aug[0:h, 384:B] = tiles(hi, 0)
         for i in range(2):
-            aug[h:B, h + i * NB:h + (i + 1) * NB] = hi[:, 1 + i, :]
+            aug[h:B, h + i * NB:h + (i + 1) * NB] = tiles(hi, 1 + i)
 
     @pl.when(which[0] == 0)
     def _():
@@ -194,7 +198,7 @@
 def gram(which, panel, partner):
     return pl.pallas_call(
         gram_kernel,
-        out_shape=jax.ShapeDtypeStruct((B // 2, 3, NB), F32),
+        out_shape=jax.ShapeDtypeStruct((B // 16, 24, NB), F32),
         in_specs=[SM, VM, VM],
         out_specs=VM,
         name="gram",
@@ -236,9 +240,9 @@
 
 def per_device(panel, trailing):
     high = lax.Precision.HIGH
-    axes, plane = ("x", "y", "z"), ("x", "y")
-    everyone, ring, depth = lax.axis_size(axes), lax.axis_size(plane), lax.axis_size("z")
-    total_rows = panel.shape[0] * everyone * 2
+    plane = ("x", "y")
+    ring, depth = lax.axis_size(plane), lax.axis_size("z")
+    total_rows = panel.shape[0] * ring * depth * 2
     core = lax.axis_index("c")
     place = lax.axis_index("z")
     swap = [(0, 1), (1, 0)]
@@ -258,9 +262,10 @@
 
     partner = lax.ppermute(panel, "c", swap)
     half = gram(which, panel, partner)
-    pieces = lax.all_to_all(half.reshape((everyone, -1) + half.shape[2:]) if everyone != h else half, axes, 0, 0, tiled=True)
+    pieces = lax.all_to_all(half.reshape(ring, -1, NB), plane, 0, 0, tiled=True)
     own = jnp.sum(pieces, axis=0)
-    mine = spread(own, axes, everyone).reshape(half.shape)
+    own = jnp.sum(spread(own, "z", depth).reshape((depth,) + own.shape), axis=0)
+    mine = spread(own, plane, ring).reshape(half.shape)
     other = lax.ppermute(mine, "c", swap)
     top, top_inverse, tail = factor_top(which, mine, other, total_rows)
     upper, inverse = factor_low(top, top_inverse, tail, total_rows)

time: 194 us -> 173 us (0.89)
  waiting for transfers between devices: 50.4 us -> 36.8 us
  starting transfers between devices: 89.3 us -> 82.5 us
    ppermute x4, waiting for transfers between devices: 18.1 us -> 8.01 us  [per_device(): lax.ppermute(forth, 'z', [(i, (i + 1) % depth) for i in range(depth)])]
    all_to_all x1, starting transfers between devices: 17.3 us -> 9.67 us  [per_device(): pieces = lax.all_to_all(half.reshape(ring, -1, NB), plane, 0, 0, tiled=True)]
    all_to_all x2 -> x3, starting transfers between devices: 21.6 us -> 19.8 us  [spread(): return lax.all_to_all(copies, axes, 0, 0, tiled=True)]
    all_to_all x2 -> x3, waiting for transfers between devices: 15.8 us -> 14.5 us  [spread(): return lax.all_to_all(copies, axes, 0, 0, tiled=True)]
  transfers between devices with their start and end apart: 15 -> 16, of which waited for: 7 -> 7; matrix products, arithmetic and copies ran while one was open for 7% -> 8% of each run, Pallas kernels for 17% -> 18%
where the time goes in v1:
time: 173 us; the launch traced here: 172 us
  starting transfers between devices  82.5 us (48%)
  waiting for transfers between devices  36.8 us (21%)
  Pallas kernels  31.8 us (18%)
  matrix products  13.5 us (8%)
  local copies, waits for them, and re-layouts  5.23 us (3%)
    all_to_all x3, starting transfers between devices, spread(): return lax.all_to_all(copies, axes, 0, 0, tiled=True)  19.8 us
    pallas_call x1, Pallas kernels, factor_top(): pl.pallas_call(functools.partial(top_kernel, 1.0 / math.sqrt(total_rows))...  15.5 us
    ppermute x3, starting transfers between devices, per_device(): back = lax.ppermute(back, 'z', [(i, (i - 1) % depth) for i in range(depth)])  14.5 us
    all_to_all x3, waiting for transfers between devices, spread(): return lax.all_to_all(copies, axes, 0, 0, tiled=True)  14.5 us
    pallas_call x1, Pallas kernels, factor_low(): pl.pallas_call(functools.partial(low_kernel, 1.0 / math.sqrt(total_rows))...  13.7 us
    dot_general x6, matrix products, dot(): lax.dot_general(a, b, (dims, ((), ())), precision=precision, preferred_el...  13.5 us
    all_to_all x1, waiting for transfers between devices, per_device(): lax.all_to_all((keep + got).reshape(ring, h // ring, -1), plane, 0, 0, ti...  12.9 us
    all_to_all x1, starting transfers between devices, per_device(): pieces = lax.all_to_all(half.reshape(ring, -1, NB), plane, 0, 0, tiled=True)  9.67 us
  transfers between devices with their start and end apart: 16, of which 7 were waited for; matrix products, arithmetic and copies ran while one was open for 8% of the time, Pallas kernels for 18%

profile of v1, /device:TPU:1, one launch (start us, length us, event | category | flops | bytes accessed | tf_op | source)
XLA Modules:
  0.0 172.0 jit_solution(5184892945941852350)
XLA Ops:
  0.6 0.0 copy-start.2
  0.6 8.9 %collective-permute-start = (f32[96,512]{1,0:T(8,128)}, f32[96,512]{1,0:T(8,128)S(1)}, u32[]{:S(2)}, u32[]{:S(2)}) collective-permute-start(f32[96,512]{1,0:T(8,128)} %a_ref.1), channel_id=1, source_target_pairs={{0,8},{8,0},{1,9},{9,1},{2,10},{10,2},{3,11},{11,3},{4,12},{12,4},... | collective-permute-start | bytes 589832 | tf_op jit(solution)/shard_map/ppermute | solution.py:263
  9.5 1.9 %collective-permute-start.2 = (f32[96,512]{1,0:T(8,128)}, f32[96,512]{1,0:T(8,128)}, u32[]{:S(2)}, u32[]{:S(2)}) collective-permute-start(f32[96,512]{1,0:T(8,128)} %a_ref.1), channel_id=1, source_target_pairs={{0,1},{1,2},{2,3},{3,4},{4,5},{5,6},{6,7},{7,0},{8,9},{9,10},{10,1... | collective-permute-start | bytes 589832 | tf_op jit(solution)/shard_map/ppermute | solution.py:257
  11.5 5.3 %collective-permute-start.3 = (f32[96,512]{1,0:T(8,128)}, f32[96,512]{1,0:T(8,128)}, u32[]{:S(2)}, u32[]{:S(2)}) collective-permute-start(f32[96,512]{1,0:T(8,128)} %a_ref.1), channel_id=1, source_target_pairs={{0,7},{1,0},{2,1},{3,2},{4,3},{5,4},{6,5},{7,6},{8,15},{9,8},{10,9... | collective-permute-start | bytes 589832 | tf_op jit(solution)/shard_map/ppermute | solution.py:260
  16.9 0.2 broadcast_in_dim.13
  17.1 0.0 copy-start.3
  17.2 0.7 copy-done.3
  17.8 2.6 %gram.1 = f32[32,24,128]{2,1,0:T(8,128)} custom-call(s32[1]{0:T(128)} %bitcast.which, f32[96,512]{1,0:T(8,128)} %a_ref.1, f32[96,512]{1,0:T(8,128)} %copy-done.3), custom_call_target="tpu_custom_call" | custom-call | tf_op jit(solution)/shard_map/gram/pallas_call | solution.py:199
  20.4 9.7 %all-to-all-start = ((f32[32,24,128]{2,1,0:T(8,128)}), f32[32,24,128]{2,1,0:T(8,128)S(1)}, u32[]{:S(2)}, u32[]{:S(2)}) async-start(f32[32,24,128]{2,1,0:T(8,128)} %gram.1), calls=%async_computation | async-start | bytes 786432 | tf_op jit(solution)/shard_map/all_to_all | solution.py:265
  30.1 0.0 copy-start
  30.1 0.0 collective-permute-done.2
  30.1 2.1 %collective-permute-start.4 = (f32[96,512]{1,0:T(8,128)}, f32[96,512]{1,0:T(8,128)S(1)}, u32[]{:S(2)}, u32[]{:S(2)}) collective-permute-start(f32[96,512]{1,0:T(8,128)} %collective-permute-done.2), channel_id=1, source_target_pairs={{0,1},{1,2},{2,3},{3,4},{4,5},{5,6},{6,7},{7,0},{8,9},{9,10},{10,1... | collective-permute-start | bytes 589832 | tf_op jit(solution)/shard_map/ppermute | solution.py:257
  32.2 0.0 collective-permute-done.3
  32.2 4.6 %collective-permute-start.5 = (f32[96,512]{1,0:T(8,128)}, f32[96,512]{1,0:T(8,128)S(1)}, u32[]{:S(2)}, u32[]{:S(2)}) collective-permute-start(f32[96,512]{1,0:T(8,128)} %collective-permute-done.3), channel_id=1, source_target_pairs={{0,7},{1,0},{2,1},{3,2},{4,3},{5,4},{6,5},{7,6},{8,15},{9,8},{10,9... | collective-permute-start | bytes 589832 | tf_op jit(solution)/shard_map/ppermute | solution.py:260
  36.8 0.9 constant_dynamic-update-slice_fusion.6
  37.7 0.9 constant_dynamic-update-slice_fusion.5
  38.7 0.8 collective-permute-done.4
  39.5 1.9 %collective-permute-start.6 = (f32[96,512]{1,0:T(8,128)S(1)}, f32[96,512]{1,0:T(8,128)S(1)}, u32[]{:S(2)}, u32[]{:S(2)}) collective-permute-start(f32[96,512]{1,0:T(8,128)S(1)} %collective-permute-done.4), channel_id=1, source_target_pairs={{0,1},{1,2},{2,3},{3,4},{4,5},{5,6},{6,7},{7,0},{8,9},{9,10},{10,1... | collective-permute-start | bytes 589832 | tf_op jit(solution)/shard_map/ppermute | solution.py:257
  41.4 0.0 collective-permute-done.5
  41.4 4.6 %collective-permute-start.7 = (f32[96,512]{1,0:T(8,128)S(1)}, f32[96,512]{1,0:T(8,128)S(1)}, u32[]{:S(2)}, u32[]{:S(2)}) collective-permute-start(f32[96,512]{1,0:T(8,128)S(1)} %collective-permute-done.5), channel_id=1, source_target_pairs={{0,7},{1,0},{2,1},{3,2},{4,3},{5,4},{6,5},{7,6},{8,15},{9,8},{10,9... | collective-permute-start | bytes 589832 | tf_op jit(solution)/shard_map/ppermute | solution.py:260
  46.0 1.6 collective-permute-done.6
  47.6 1.9 %collective-permute-start.8 = (f32[96,512]{1,0:T(8,128)S(1)}, f32[96,512]{1,0:T(8,128)S(1)}, u32[]{:S(2)}, u32[]{:S(2)}) collective-permute-start(f32[96,512]{1,0:T(8,128)S(1)} %collective-permute-done.6), channel_id=1, source_target_pairs={{0,1},{1,2},{2,3},{3,4},{4,5},{5,6},{6,7},{7,0},{8,9},{9,10},{10,1... | collective-permute-start | bytes 589832 | tf_op jit(solution)/shard_map/ppermute | solution.py:257
  49.6 0.0 collective-permute-done.7
  49.6 5.6 %collective-permute-done.8 = f32[96,512]{1,0:T(8,128)S(1)} collective-permute-done((f32[96,512]{1,0:T(8,128)S(1)}, f32[96,512]{1,0:T(8,128)S(1)}, u32[]{:S(2)}, u32[]{:S(2)}) %collective-permute-start.8) | collective-permute-done | bytes 196640 | tf_op jit(solution)/shard_map/ppermute | solution.py:257
  55.3 1.6 fusion.1
  56.9 5.4 %collective-permute-start.9 = (f32[256,512]{1,0:T(8,128)}, f32[256,512]{1,0:T(8,128)}, u32[]{:S(2)}, u32[]{:S(2)}) collective-permute-start(f32[256,512]{1,0:T(8,128)} %fusion.1), channel_id=1, source_target_pairs={{0,8},{8,0},{1,9},{9,1},{2,10},{10,2},{3,11},{11,3},{4,12},{12,4},... | collective-permute-start | bytes 1572872 | tf_op jit(solution)/shard_map/ppermute | solution.py:274
  62.3 0.0 all-to-all-done
  62.4 0.6 broadcast_in_dim.11
  63.0 3.7 %all-to-all-start.1 = ((f32[8,24,128]{2,1,0:T(8,128)}), f32[8,24,128]{2,1,0:T(8,128)S(1)}, u32[]{:S(2)}, u32[]{:S(2)}) async-start(f32[8,24,128]{2,1,0:T(8,128)} %broadcast_in_dim.11), calls=%async_computation.1 | async-start | bytes 196608 | tf_op jit(solution)/shard_map/all_to_all | solution.py:238
  66.7 2.7 %fusion = f32[32,8,512]{2,1,0:T(8,128)} fusion(f32[256,512]{1,0:T(8,128)} %collective-permute-done.9, f32[768,512]{1,0:T(8,128)S(1)} %copy-done, f32[768,512]{1,0:T(8,128)S(1)} %constant_dynamic-update-slice_fusion, s32[]{:T(128)S(6)} %select_n.78), kind=kOutput, calls=%fused_computation.3 | convolution fusion | flops 604110848 | bytes 3407876 | tf_op jit(solution)/shard_map/dot_general | solution.py:233
  69.4 5.0 %all-to-all-done.1 = f32[8,24,128]{2,1,0:T(8,128)S(1)} async-done(((f32[8,24,128]{2,1,0:T(8,128)}), f32[8,24,128]{2,1,0:T(8,128)S(1)}, u32[]{:S(2)}, u32[]{:S(2)}) %all-to-all-start.1) | async-done | bytes 98336 | tf_op jit(solution)/shard_map/all_to_all | solution.py:238
  74.4 9.4 %all-to-all-start.3 = ((f32[32,8,512]{2,1,0:T(8,128)}), f32[32,8,512]{2,1,0:T(8,128)}, u32[]{:S(2)}, u32[]{:S(2)}) async-start(f32[32,8,512]{2,1,0:T(8,128)} %fusion), calls=%async_computation.3 | async-start | bytes 1048576 | tf_op jit(solution)/shard_map/all_to_all | solution.py:276
  83.8 12.9 %all-to-all-done.3 = f32[32,8,512]{2,1,0:T(8,128)} async-done(((f32[32,8,512]{2,1,0:T(8,128)}), f32[32,8,512]{2,1,0:T(8,128)}, u32[]{:S(2)}, u32[]{:S(2)}) %all-to-all-start.3) | async-done | bytes 524320 | tf_op jit(solution)/shard_map/all_to_all | solution.py:276
  96.7 0.8 broadcast_in_dim.12
  97.5 8.6 %all-to-all-start.2 = ((f32[32,24,128]{2,1,0:T(8,128)}), f32[32,24,128]{2,1,0:T(8,128)S(1)}, u32[]{:S(2)}, u32[]{:S(2)}) async-start(f32[32,24,128]{2,1,0:T(8,128)} %broadcast_in_dim.12), calls=%async_computation.2 | async-start | bytes 786432 | tf_op jit(solution)/shard_map/all_to_all | solution.py:238
  106.1 1.1 reduce_sum.29
  107.2 9.4 %all-to-all-done.2.mine_ref = f32[32,24,128]{2,1,0:T(8,128)S(1)} async-done(((f32[32,24,128]{2,1,0:T(8,128)}), f32[32,24,128]{2,1,0:T(8,128)S(1)}, u32[]{:S(2)}, u32[]{:S(2)}) %all-to-all-start.2) | async-done | bytes 393248 | tf_op jit(solution)/shard_map/all_to_all | solution.py:238
  116.6 0.9 broadcast_in_dim.28
  117.6 7.5 %all-to-all-start.4 = ((f32[32,8,512]{2,1,0:T(8,128)}), f32[32,8,512]{2,1,0:T(8,128)}, u32[]{:S(2)}, u32[]{:S(2)}) async-start(f32[32,8,512]{2,1,0:T(8,128)} %broadcast_in_dim.28), calls=%async_computation.4 | async-start | bytes 1048576 | tf_op jit(solution)/shard_map/all_to_all | solution.py:238
  125.1 4.6 %collective-permute-start.1 = (f32[32,24,128]{2,1,0:T(8,128)S(1)}, f32[32,24,128]{2,1,0:T(8,128)}, u32[]{:S(2)}, u32[]{:S(2)}) collective-permute-start(f32[32,24,128]{2,1,0:T(8,128)S(1)} %all-to-all-done.2.mine_ref), channel_id=1, source_target_pairs={{0,8},{8,0},{1,9},{9,1},{2,10},{10,2},{3,11},{11,3},{4,12},{12,4},... | collective-permute-start | bytes 1179656 | tf_op jit(solution)/shard_map/ppermute | solution.py:269
  129.7 1.5 collective-permute-done.1.other_ref
  131.2 15.5 %factor_top.1 = (f32[256,512]{1,0:T(8,128)}, f32[256,256]{1,0:T(8,128)}, f32[256,512]{1,0:T(8,128)}) custom-call(s32[1]{0:T(128)} %bitcast.which, f32[32,24,128]{2,1,0:T(8,128)} %copy-done.1, f32[32,24,128]{2,1,0:T(8,128)} %collective-permute-done.1.other_ref), custom_call_target="tpu_custom_call" | custom-call | tf_op jit(solution)/shard_map/factor_top/pallas_call | solution.py:210
  146.7 13.7 %factor_low.1 = (f32[512,512]{1,0:T(8,128)}, f32[512,512]{1,0:T(8,128)}) custom-call(f32[256,512]{1,0:T(8,128)} %get-tuple-element.7.top_ref, f32[256,256]{1,0:T(8,128)} %get-tuple-element.8.mtop_ref, f32[256,512]{1,0:T(8,128)} %get-tuple-element.9.tail_ref), custom_call_target="tpu_custom_call" | custom-call | tf_op jit(solution)/shard_map/factor_low/pallas_call | solution.py:222
  160.3 2.5 %collective-permute-start.10 = (f32[256,512]{1,0:T(8,128)}, f32[256,512]{1,0:T(8,128)S(1)}, u32[]{:S(2)}, u32[]{:S(2)}) collective-permute-start(f32[256,512]{1,0:T(8,128)} %bitcast.2), channel_id=1, source_target_pairs={{0,8},{8,0},{1,9},{9,1},{2,10},{10,2},{3,11},{11,3},{4,12},{12,4},... | collective-permute-start | bytes 1572872 | tf_op jit(solution)/shard_map/ppermute | solution.py:279
  162.8 3.4 %fusion.12 = f32[512,512]{1,0:T(8,128)S(1)} fusion(f32[512,512]{1,0:T(8,128)} %get-tuple-element.11), kind=kOutput, calls=%fused_computation.23 | convolution fusion | flops 1610612736 | bytes 2097152 | tf_op jit(solution)/shard_map/dot_general | solution.py:233
  166.3 2.1 %fusion.5 = f32[512,512]{1,0:T(8,128)S(1)} fusion(f32[512,512]{1,0:T(8,128)S(1)} %fusion.12, s32[]{:T(128)S(6)} %select_n.78, f32[32,8,512]{2,1,0:T(8,128)} %all-to-all-done.4), kind=kOutput, calls=%fused_computation.8 | convolution fusion | flops 805306368 | bytes 2097156 | tf_op jit(solution)/shard_map/dot_general | solution.py:233
  168.4 1.1 convolution_add_fusion
  169.4 2.6 %convolution_subtract_fusion = f32[768,512]{1,0:T(8,128)} fusion(f32[768,512]{1,0:T(8,128)S(1)} %copy-done, f32[768,512]{1,0:T(8,128)S(1)} %constant_dynamic-update-slice_fusion, f32[512,512]{1,0:T(8,128)S(1)} %convolution_add_fusion), kind=kOutput, calls=%fused_computation | convolution fusion | flops 1208352768 | bytes 5767168 | tf_op jit(solution)/shard_map/dot_general | solution.py:233
  (16 shorter events, 0.2 us)
Async XLA Ops:
  0.6 16.5 %copy-start.2 = (f32[96,512]{1,0:T(8,128)S(1)}, f32[96,512]{1,0:T(8,128)}, u32[]{:S(2)}) copy-start(f32[96,512]{1,0:T(8,128)} %a_ref.1) | copy-start | bytes 589828
  0.6 16.5 %collective-permute-start = (f32[96,512]{1,0:T(8,128)}, f32[96,512]{1,0:T(8,128)S(1)}, u32[]{:S(2)}, u32[]{:S(2)}) collective-permute-start(f32[96,512]{1,0:T(8,128)} %a_ref.1), channel_id=1, source_target_pairs={{0,8},{8,0},{1,9},{9,1},{2,10},{10,2},{3,11},{11,3},{4,12},{12,4},... | collective-permute-start | bytes 589832 | tf_op jit(solution)/shard_map/ppermute | solution.py:263
  9.5 20.6 %collective-permute-start.2 = (f32[96,512]{1,0:T(8,128)}, f32[96,512]{1,0:T(8,128)}, u32[]{:S(2)}, u32[]{:S(2)}) collective-permute-start(f32[96,512]{1,0:T(8,128)} %a_ref.1), channel_id=1, source_target_pairs={{0,1},{1,2},{2,3},{3,4},{4,5},{5,6},{6,7},{7,0},{8,9},{9,10},{10,1... | collective-permute-start | bytes 589832 | tf_op jit(solution)/shard_map/ppermute | solution.py:257
  11.5 20.7 %collective-permute-start.3 = (f32[96,512]{1,0:T(8,128)}, f32[96,512]{1,0:T(8,128)}, u32[]{:S(2)}, u32[]{:S(2)}) collective-permute-start(f32[96,512]{1,0:T(8,128)} %a_ref.1), channel_id=1, source_target_pairs={{0,7},{1,0},{2,1},{3,2},{4,3},{5,4},{6,5},{7,6},{8,15},{9,8},{10,9... | collective-permute-start | bytes 589832 | tf_op jit(solution)/shard_map/ppermute | solution.py:260
  17.1 0.7 copy-start.3
  20.4 41.9 %all-to-all-start = ((f32[32,24,128]{2,1,0:T(8,128)}), f32[32,24,128]{2,1,0:T(8,128)S(1)}, u32[]{:S(2)}, u32[]{:S(2)}) async-start(f32[32,24,128]{2,1,0:T(8,128)} %gram.1), calls=%async_computation | async-start | bytes 786432 | tf_op jit(solution)/shard_map/all_to_all | solution.py:265
  30.1 25.2 %copy-start = (f32[768,512]{1,0:T(8,128)S(1)}, f32[768,512]{1,0:T(8,128)}, u32[]{:S(2)}) copy-start(f32[768,512]{1,0:T(8,128)} %param.3) | copy-start | bytes 4718596
  30.1 9.4 %collective-permute-start.4 = (f32[96,512]{1,0:T(8,128)}, f32[96,512]{1,0:T(8,128)S(1)}, u32[]{:S(2)}, u32[]{:S(2)}) collective-permute-start(f32[96,512]{1,0:T(8,128)} %collective-permute-done.2), channel_id=1, source_target_pairs={{0,1},{1,2},{2,3},{3,4},{4,5},{5,6},{6,7},{7,0},{8,9},{9,10},{10,1... | collective-permute-start | bytes 589832 | tf_op jit(solution)/shard_map/ppermute | solution.py:257
  32.2 9.2 %collective-permute-start.5 = (f32[96,512]{1,0:T(8,128)}, f32[96,512]{1,0:T(8,128)S(1)}, u32[]{:S(2)}, u32[]{:S(2)}) collective-permute-start(f32[96,512]{1,0:T(8,128)} %collective-permute-done.3), channel_id=1, source_target_pairs={{0,7},{1,0},{2,1},{3,2},{4,3},{5,4},{6,5},{7,6},{8,15},{9,8},{10,9... | collective-permute-start | bytes 589832 | tf_op jit(solution)/shard_map/ppermute | solution.py:260
  39.5 8.1 %collective-permute-start.6 = (f32[96,512]{1,0:T(8,128)S(1)}, f32[96,512]{1,0:T(8,128)S(1)}, u32[]{:S(2)}, u32[]{:S(2)}) collective-permute-start(f32[96,512]{1,0:T(8,128)S(1)} %collective-permute-done.4), channel_id=1, source_target_pairs={{0,1},{1,2},{2,3},{3,4},{4,5},{5,6},{6,7},{7,0},{8,9},{9,10},{10,1... | collective-permute-start | bytes 589832 | tf_op jit(solution)/shard_map/ppermute | solution.py:257
  41.4 8.2 %collective-permute-start.7 = (f32[96,512]{1,0:T(8,128)S(1)}, f32[96,512]{1,0:T(8,128)S(1)}, u32[]{:S(2)}, u32[]{:S(2)}) collective-permute-start(f32[96,512]{1,0:T(8,128)S(1)} %collective-permute-done.5), channel_id=1, source_target_pairs={{0,7},{1,0},{2,1},{3,2},{4,3},{5,4},{6,5},{7,6},{8,15},{9,8},{10,9... | collective-permute-start | bytes 589832 | tf_op jit(solution)/shard_map/ppermute | solution.py:260
  47.6 7.6 %collective-permute-start.8 = (f32[96,512]{1,0:T(8,128)S(1)}, f32[96,512]{1,0:T(8,128)S(1)}, u32[]{:S(2)}, u32[]{:S(2)}) collective-permute-start(f32[96,512]{1,0:T(8,128)S(1)} %collective-permute-done.6), channel_id=1, source_target_pairs={{0,1},{1,2},{2,3},{3,4},{4,5},{5,6},{6,7},{7,0},{8,9},{9,10},{10,1... | collective-permute-start | bytes 589832 | tf_op jit(solution)/shard_map/ppermute | solution.py:257
  56.9 9.8 %collective-permute-start.9 = (f32[256,512]{1,0:T(8,128)}, f32[256,512]{1,0:T(8,128)}, u32[]{:S(2)}, u32[]{:S(2)}) collective-permute-start(f32[256,512]{1,0:T(8,128)} %fusion.1), channel_id=1, source_target_pairs={{0,8},{8,0},{1,9},{9,1},{2,10},{10,2},{3,11},{11,3},{4,12},{12,4},... | collective-permute-start | bytes 1572872 | tf_op jit(solution)/shard_map/ppermute | solution.py:274
  63.0 11.4 %all-to-all-start.1 = ((f32[8,24,128]{2,1,0:T(8,128)}), f32[8,24,128]{2,1,0:T(8,128)S(1)}, u32[]{:S(2)}, u32[]{:S(2)}) async-start(f32[8,24,128]{2,1,0:T(8,128)} %broadcast_in_dim.11), calls=%async_computation.1 | async-start | bytes 196608 | tf_op jit(solution)/shard_map/all_to_all | solution.py:238
  74.4 22.2 %all-to-all-start.3 = ((f32[32,8,512]{2,1,0:T(8,128)}), f32[32,8,512]{2,1,0:T(8,128)}, u32[]{:S(2)}, u32[]{:S(2)}) async-start(f32[32,8,512]{2,1,0:T(8,128)} %fusion), calls=%async_computation.3 | async-start | bytes 1048576 | tf_op jit(solution)/shard_map/all_to_all | solution.py:276
  97.5 19.2 %all-to-all-start.2 = ((f32[32,24,128]{2,1,0:T(8,128)}), f32[32,24,128]{2,1,0:T(8,128)S(1)}, u32[]{:S(2)}, u32[]{:S(2)}) async-start(f32[32,24,128]{2,1,0:T(8,128)} %broadcast_in_dim.12), calls=%async_computation.2 | async-start | bytes 786432 | tf_op jit(solution)/shard_map/all_to_all | solution.py:238
  116.6 14.5 %copy-start.1 = (f32[32,24,128]{2,1,0:T(8,128)}, f32[32,24,128]{2,1,0:T(8,128)S(1)}, u32[]{:S(2)}) copy-start(f32[32,24,128]{2,1,0:T(8,128)S(1)} %all-to-all-done.2.mine_ref) | copy-start | bytes 1179652
  117.6 42.8 %all-to-all-start.4 = ((f32[32,8,512]{2,1,0:T(8,128)}), f32[32,8,512]{2,1,0:T(8,128)}, u32[]{:S(2)}, u32[]{:S(2)}) async-start(f32[32,8,512]{2,1,0:T(8,128)} %broadcast_in_dim.28), calls=%async_computation.4 | async-start | bytes 1048576 | tf_op jit(solution)/shard_map/all_to_all | solution.py:238
  125.1 6.0 %collective-permute-start.1 = (f32[32,24,128]{2,1,0:T(8,128)S(1)}, f32[32,24,128]{2,1,0:T(8,128)}, u32[]{:S(2)}, u32[]{:S(2)}) collective-permute-start(f32[32,24,128]{2,1,0:T(8,128)S(1)} %all-to-all-done.2.mine_ref), channel_id=1, source_target_pairs={{0,8},{8,0},{1,9},{9,1},{2,10},{10,2},{3,11},{11,3},{4,12},{12,4},... | collective-permute-start | bytes 1179656 | tf_op jit(solution)/shard_map/ppermute | solution.py:269
  160.3 8.0 %collective-permute-start.10 = (f32[256,512]{1,0:T(8,128)}, f32[256,512]{1,0:T(8,128)S(1)}, u32[]{:S(2)}, u32[]{:S(2)}) collective-permute-start(f32[256,512]{1,0:T(8,128)} %bitcast.2), channel_id=1, source_target_pairs={{0,8},{8,0},{1,9},{9,1},{2,10},{10,2},{3,11},{11,3},{4,12},{12,4},... | collective-permute-start | bytes 1572872 | tf_op jit(solution)/shard_map/ppermute | solution.py:279

commit v2 on v1

v2 whole, which is shorter than its diff:
```python
import functools
import math

import jax
import jax.numpy as jnp
from jax import lax
from jax.experimental import pallas as pl
from jax.experimental.pallas import tpu as pltpu
from jax.sharding import Mesh, PartitionSpec as P


HI = lax.Precision.HIGHEST
B = 512
NB = 128
F32 = jnp.float32


def gram_kernel(which, a_ref, b_ref, out_ref):
    h = B // 2

    def prod(rows, cols):
        total = None
        for ref in (a_ref, b_ref):
            term = lax.dot_general(
                ref[:, rows], ref[:, cols], (((0,), (0,)), ((), ())), precision=HI, preferred_element_type=F32
            )
            total = term if total is None else total + term
        return total

    def put(j, v):
        for i in range(v.shape[1] // NB):
            tiles = v[:, i * NB:(i + 1) * NB].reshape(h // 8, 8, NB)
            out_ref[:, 8 * (j + i):8 * (j + i + 1), :] = tiles

    @pl.when(which[0] == 0)
    def _():
        put(0, prod(slice(0, h), slice(0, 384)))

    @pl.when(which[0] != 0)
    def _():
        put(0, prod(slice(0, h), slice(384, B)))
        put(1, prod(slice(h, B), slice(h, B)))


def sub_row(v, j):
    return jnp.broadcast_to(v[j:j + 1, :], v.shape)


def tree(p):
    return ((p[0] + p[1]) + (p[2] + p[3])) + ((p[4] + p[5]) + (p[6] + p[7]))


def solve_strip(a, y, cols, sub):
    rows_r = rows_y = jnp.zeros_like(a)
    for j in range(0, 8, 2):
        h0, h1 = sub == j, sub == j + 1
        c0, c1 = cols[j], cols[j + 1]
        d0, b, d1 = sub_row(c0, j), sub_row(c1, j), sub_row(c1, j + 1)
        det = d0 * d1 - b * b
        rdet = 1.0 / det
        r0 = lax.rsqrt(d0)
        r1 = lax.rsqrt(det) * (d0 * r0)
        g = b * (r0 * r0)
        e0 = jnp.where(h0, -d1, jnp.where(h1, b, c0 * d1 - c1 * b))
        e1 = jnp.where(h0, b, jnp.where(h1, -d0, c1 * d0 - c0 * b))
        pair = h0 | h1

        def apply(v):
            v0, v1 = sub_row(v, j), sub_row(v, j + 1)
            return jnp.where(pair, 0.0, v) - (e0 * v0 + e1 * v1) * rdet, v0, v1

        a, a0, a1 = apply(a)
        y, y0, y1 = apply(y)
        rows_r = jnp.where(h0, a0 * r0, jnp.where(h1, (a1 - g * a0) * r1, rows_r))
        rows_y = jnp.where(h0, y0 * r0, jnp.where(h1, (y1 - g * y0) * r1, rows_y))
        for m in range(j + 2, 8):
            cols[m] = apply(cols[m])[0]
    return a, y, rows_r, rows_y


def factor_block(aug, inv, at):
    sub = lax.broadcasted_iota(jnp.int32, (8, NB), 0)
    lane = lax.broadcasted_iota(jnp.int32, (8, NB), 1)
    strips = range(NB // 8)
    a = [aug[at + 8 * t:at + 8 * t + 8, at:at + NB] for t in strips]
    y = [jnp.where(lane == sub + 8 * t, 1.0, 0.0).astype(F32) for t in strips]
    for s in strips:
        lanes = [slice(8 * s + j, 8 * s + j + 1) for j in range(8)]
        cols = [jnp.broadcast_to(a[s][:, c], (8, NB)) for c in lanes]
        av, yv, rows_r, rows_y = solve_strip(a[s], y[s], cols, sub)
        inv[8 * s:8 * s + 8, :] = rows_y
        inv[NB + 8 * s:NB + 8 * s + 8, :] = rows_r
        va = [sub_row(av, j) for j in range(8)]
        vy = [sub_row(yv, j) for j in range(8)]
        for t in range(s + 1, NB // 8):
            left = [jnp.broadcast_to(a[t][:, c], (8, NB)) for c in lanes]
            a[t] = a[t] - tree([u * v for u, v in zip(left, va)])
            y[t] = y[t] - tree([u * v for u, v in zip(left, vy)])


def run_block(aug, inv, at, width, done):
    factor_block(aug, inv, at)
    rows = slice(at, at + NB)
    end = width + done
    aug[rows, at + NB:end] = jnp.dot(
        inv[0:NB, :], aug[rows, at + NB:end], precision=HI, preferred_element_type=F32
    )
    aug[rows, end:end + NB] = inv[0:NB, :]
    for low in range(at + NB, width, NB):
        aug[low:low + NB, low:end + NB] -= lax.dot_general(
            aug[rows, low:low + NB], aug[rows, low:end + NB],
            (((0,), (0,)), ((), ())), precision=HI, preferred_element_type=F32,
        )


def triangle(inv):
    r = lax.broadcasted_iota(jnp.int32, (NB, NB), 0)
    c = lax.broadcasted_iota(jnp.int32, (NB, NB), 1)
    return jnp.where(c >= r, inv[NB:2 * NB, :], 0.0)


def top_kernel(scale, which, mine_ref, other_ref, r_out, m_out, tail_out, s_out, aug, inv):
    h = B // 2

    def load(lo, hi):
        def tiles(ref, i):
            return ref[:, 8 * i:8 * i + 8, :].reshape(h, NB)

        for i in range(3):
            aug[0:h, i * NB:(i + 1) * NB] = tiles(lo, i)
        aug[0:h, 384:B] = tiles(hi, 0)
        for i in range(2):
            aug[h:B, h + i * NB:h + (i + 1) * NB] = tiles(hi, 1 + i)

    @pl.when(which[0] == 0)
    def _():
        load(mine_ref, other_ref)

    @pl.when(which[0] != 0)
    def _():
        load(other_ref, mine_ref)

    eye = lax.broadcasted_iota(jnp.int32, (NB, NB), 0) == lax.broadcasted_iota(jnp.int32, (NB, NB), 1)
    col = []
    for at in range(0, B, NB):
        diag = jnp.where(eye, aug[at:at + NB, at:at + NB], 0.0)
        row = jnp.sum(diag, axis=0, keepdims=True)
        s_out[0:1, at:at + NB] = lax.rsqrt(row)
        s_out[1:2, at:at + NB] = row * lax.rsqrt(row) * scale
        col.append(lax.rsqrt(jnp.sum(diag, axis=1, keepdims=True)))
    for b in range(B // NB):
        rows, cols = slice(b * NB, (b + 1) * NB), slice(b * NB, B)
        aug[rows, cols] = aug[rows, cols] * col[b] * s_out[0:1, cols]
    aug[:, B:] = jnp.zeros((B, h), F32)

    for at in (0, NB):
        run_block(aug, inv, at, B, at)
        rows = slice(at, at + NB)
        r_out[rows, at:at + NB] = triangle(inv) * s_out[1:2, at:at + NB]
        r_out[rows, at + NB:B] = aug[rows, at + NB:B] * s_out[1:2, at + NB:B]
        m_out[rows, :] = aug[rows, B:] * s_out[0:1, 0:h]
    r_out[NB:h, 0:NB] = jnp.zeros((NB, NB), F32)
    tail_out[...] = aug[h:B, h:]


def low_kernel(top_ref, mtop_ref, tail_ref, s_ref, r_out, g_out, aug, inv, low):
    h = B // 2
    r_out[0:h, :] = top_ref[...]
    r_out[h:B, 0:h] = jnp.zeros((h, h), F32)
    aug[:, 0:B] = tail_ref[...]
    aug[:, B:] = jnp.zeros((h, h), F32)
    for at in (0, NB):
        run_block(aug, inv, at, h, h + at)
        rows = slice(at, at + NB)
        g = h + at
        r_out[g:g + NB, g:g + NB] = triangle(inv) * s_ref[1:2, g:g + NB]
        if g + NB < B:
            r_out[g:g + NB, g + NB:B] = aug[rows, at + NB:h] * s_ref[1:2, g + NB:B]
        low[rows, :] = aug[rows, h:] * s_ref[0:1, :]
    r_out[B - NB:B, h:B - NB] = jnp.zeros((NB, NB), F32)

    def square(a, b):
        return lax.dot_general(a, b, (((0,), (0,)), ((), ())), precision=HI, preferred_element_type=F32)

    g_out[0:h, 0:h] = square(low[:, 0:h], low[:, 0:h]) + square(mtop_ref[...], mtop_ref[...])
    g_out[h:B, :] = square(low[:, h:B], low[...])
    g_out[0:h, h:B] = square(low[:, 0:h], low[:, h:B])


VM = pl.BlockSpec(memory_space=pltpu.VMEM)
SM = pl.BlockSpec(memory_space=pltpu.SMEM)


def gram(which, panel, partner):
    return pl.pallas_call(
        gram_kernel,
        out_shape=jax.ShapeDtypeStruct((B // 16, 24, NB), F32),
        in_specs=[SM, VM, VM],
        out_specs=VM,
        name="gram",
    )(which, panel, partner)


def factor_top(which, mine, other, total_rows):
    h = B // 2
    return pl.pallas_call(
        functools.partial(top_kernel, 1.0 / math.sqrt(total_rows)),
        out_shape=[jax.ShapeDtypeStruct(s, F32) for s in ((h, B), (h, h), (h, B), (8, B))],
        in_specs=[SM, VM, VM],
        out_specs=[VM] * 4,
        scratch_shapes=[pltpu.VMEM((B, B + h), F32), pltpu.VMEM((2 * NB, NB), F32)],
        name="factor_top",
    )(which, mine, other)


def factor_low(top, top_inverse, tail, scales):
    h = B // 2
    return pl.pallas_call(
        low_kernel,
        out_shape=[jax.ShapeDtypeStruct((B, B), F32)] * 2,
        in_specs=[VM] * 4,
        out_specs=[VM] * 2,
        scratch_shapes=[pltpu.VMEM((h, h + B), F32), pltpu.VMEM((2 * NB, NB), F32), pltpu.VMEM((h, B), F32)],
        name="factor_low",
    )(top, top_inverse, tail, scales)


def dot(a, b, dims, precision=HI):
    return lax.dot_general(a, b, (dims, ((), ())), precision=precision, preferred_element_type=jnp.float32)


def spread(own, axes, parts):
    copies = jnp.broadcast_to(own[None], (parts,) + own.shape)
    return lax.all_to_all(copies, axes, 0, 0, tiled=True)


def per_device(panel, trailing):
    high = lax.Precision.HIGH
    plane = ("x", "y")
    ring, depth = lax.axis_size(plane), lax.axis_size("z")
    total_rows = panel.shape[0] * ring * depth * 2
    core = lax.axis_index("c")
    place = lax.axis_index("z")
    swap = [(0, 1), (1, 0)]
    h = B // 2
    each = panel.shape[0]
    which = jnp.full((1,), core, jnp.int32)

    block = jnp.zeros((depth * each, B), jnp.float32)
    block = lax.dynamic_update_slice(block, panel, (place * each, 0))
    forth = back = panel
    for k in range(1, depth // 2 + 1):
        forth = lax.ppermute(forth, "z", [(i, (i + 1) % depth) for i in range(depth)])
        block = lax.dynamic_update_slice(block, forth, ((place + depth - k) % depth * each, 0))
        if k < depth - k:
            back = lax.ppermute(back, "z", [(i, (i - 1) % depth) for i in range(depth)])
            block = lax.dynamic_update_slice(block, back, ((place + k) % depth * each, 0))

    partner = lax.ppermute(panel, "c", swap)
    half = gram(which, panel, partner)
    pieces = lax.all_to_all(half.reshape(ring, -1, NB), plane, 0, 0, tiled=True)
    own = jnp.sum(pieces, axis=0)
    own = jnp.sum(spread(own, "z", depth).reshape((depth,) + own.shape), axis=0)
    mine = spread(own, plane, ring).reshape(half.shape)
    other = lax.ppermute(mine, "c", swap)
    top, top_inverse, tail, scales = factor_top(which, mine, other, total_rows)
    upper, ginv = factor_low(top, top_inverse, tail, scales)

    give = dot(lax.dynamic_slice(block, (0, (1 - core) * h), (depth * each, h)), trailing, ((0,), (0,)), high)
    got = lax.ppermute(give, "c", swap)
    keep = dot(lax.dynamic_slice(block, (0, core * h), (depth * each, h)), trailing, ((0,), (0,)), high)
    keep = lax.optimization_barrier(keep)
    pieces = lax.all_to_all((keep + got).reshape(ring, h // ring, -1), plane, 0, 0, tiled=True)
    own = jnp.sum(pieces, axis=0)
    near = spread(own, plane, ring).reshape(h, -1)
    far = lax.ppermute(near, "c", swap)

    weights = dot(lax.dynamic_slice(ginv, (core * h, 0), (h, B)), near, ((0,), (0,)))
    weights = weights + dot(lax.dynamic_slice(ginv, ((1 - core) * h, 0), (h, B)), far, ((0,), (0,)))
    residual = trailing - dot(block, weights, ((1,), (0,)), high)
    return (upper, residual)


def solution(mesh):
    row, col = mesh.devices.shape
    y = 8 if row == 64 else 2
    fine = Mesh(mesh.devices.reshape(row // (2 * y), y, 2, col), ("x", "y", "c", "z"))
    row_axes = ("x", "y", "c")
    return jax.shard_map(
        per_device,
        mesh=fine,
        in_specs=(P(row_axes + ("z",), None), P(row_axes, "z")),
        out_specs=(P(), P(row_axes, "z")),
        check_vma=False,
    )
```

time: 173 us -> 179 us (1.035)
  waiting for transfers between devices: 36.8 us -> 44.8 us
  Pallas kernels: 31.8 us -> 26.4 us
  starting transfers between devices: 82.5 us -> 86.3 us
  matrix products: 13.5 us -> 10.3 us
  other arithmetic: 1.14 us -> 3.22 us
    all_to_all x3, waiting for transfers between devices: 14.5 us -> 23.2 us  [spread(): return lax.all_to_all(copies, axes, 0, 0, tiled=True)]
    ppermute x1, starting transfers between devices: 2.5 us -> 6.9 us  [per_device(): far = lax.ppermute(near, 'c', swap)]
    pallas_call x1, Pallas kernels: 15.5 us -> 11.5 us  [factor_top(): pl.pallas_call(functools.partial(top_kernel, 1.0 / math.sqrt(total_rows))...]
    dot_general x6 -> x5, matrix products: 13.5 us -> 10.3 us  [dot(): lax.dot_general(a, b, (dims, ((), ())), precision=precision, preferred_el...]
    reshape x0 -> x1, other arithmetic: none -> 2.07 us  [per_device(): (keep + got).reshape(ring, h // ring, -1)]
  transfers between devices with their start and end apart: 16 -> 16, of which waited for: 7 -> 7; matrix products, arithmetic and copies ran while one was open for 8% -> 7% of each run, Pallas kernels for 18% -> 15%
where the time goes in v2:
time: 179 us; the launch traced here: 177 us
  starting transfers between devices  86.3 us (48%)
  waiting for transfers between devices  44.8 us (25%)
  Pallas kernels  26.4 us (15%)
  matrix products  10.3 us (6%)
  local copies, waits for them, and re-layouts  5.22 us (3%)
  other arithmetic  3.22 us (2%)
    all_to_all x3, waiting for transfers between devices, spread(): return lax.all_to_all(copies, axes, 0, 0, tiled=True)  23.2 us
    all_to_all x3, starting transfers between devices, spread(): return lax.all_to_all(copies, axes, 0, 0, tiled=True)  19.3 us
    ppermute x3, starting transfers between devices, per_device(): back = lax.ppermute(back, 'z', [(i, (i - 1) % depth) for i in range(depth)])  14.5 us
    all_to_all x1, waiting for transfers between devices, per_device(): lax.all_to_all((keep + got).reshape(ring, h // ring, -1), plane, 0, 0, ti...  13.5 us
    pallas_call x1, Pallas kernels, factor_low(): pl.pallas_call(low_kernel, out_shape=[jax.ShapeDtypeStruct((B, B), F32)]...  12.3 us
    pallas_call x1, Pallas kernels, factor_top(): pl.pallas_call(functools.partial(top_kernel, 1.0 / math.sqrt(total_rows))...  11.5 us
    dot_general x5, matrix products, dot(): lax.dot_general(a, b, (dims, ((), ())), precision=precision, preferred_el...  10.3 us
    all_to_all x1, starting transfers between devices, per_device(): pieces = lax.all_to_all(half.reshape(ring, -1, NB), plane, 0, 0, tiled=True)  9.67 us
  transfers between devices with their start and end apart: 16, of which 7 were waited for; matrix products, arithmetic and copies ran while one was open for 7% of the time, Pallas kernels for 15%

profile of v2, /device:TPU:1, one launch (start us, length us, event | category | flops | bytes accessed | tf_op | source)
XLA Modules:
  0.0 177.3 jit_solution(3889803379303364884)
XLA Ops:
  0.6 0.0 copy-start.3
  0.6 8.9 %collective-permute-start = (f32[96,512]{1,0:T(8,128)}, f32[96,512]{1,0:T(8,128)S(1)}, u32[]{:S(2)}, u32[]{:S(2)}) collective-permute-start(f32[96,512]{1,0:T(8,128)} %a_ref.1), channel_id=1, source_target_pairs={{0,8},{8,0},{1,9},{9,1},{2,10},{10,2},{3,11},{11,3},{4,12},{12,4},... | collective-permute-start | bytes 589832 | tf_op jit(solution)/shard_map/ppermute | solution.py:259
  9.5 1.9 %collective-permute-start.2 = (f32[96,512]{1,0:T(8,128)}, f32[96,512]{1,0:T(8,128)}, u32[]{:S(2)}, u32[]{:S(2)}) collective-permute-start(f32[96,512]{1,0:T(8,128)} %a_ref.1), channel_id=1, source_target_pairs={{0,1},{1,2},{2,3},{3,4},{4,5},{5,6},{6,7},{7,0},{8,9},{9,10},{10,1... | collective-permute-start | bytes 589832 | tf_op jit(solution)/shard_map/ppermute | solution.py:253
  11.5 5.3 %collective-permute-start.3 = (f32[96,512]{1,0:T(8,128)}, f32[96,512]{1,0:T(8,128)}, u32[]{:S(2)}, u32[]{:S(2)}) collective-permute-start(f32[96,512]{1,0:T(8,128)} %a_ref.1), channel_id=1, source_target_pairs={{0,7},{1,0},{2,1},{3,2},{4,3},{5,4},{6,5},{7,6},{8,15},{9,8},{10,9... | collective-permute-start | bytes 589832 | tf_op jit(solution)/shard_map/ppermute | solution.py:256
  16.9 0.2 broadcast_in_dim.13
  17.1 0.0 copy-start.4
  17.2 0.7 copy-done.4
  17.8 2.6 %gram.1 = f32[32,24,128]{2,1,0:T(8,128)} custom-call(s32[1]{0:T(128)} %bitcast.which, f32[96,512]{1,0:T(8,128)} %a_ref.1, f32[96,512]{1,0:T(8,128)} %copy-done.4), custom_call_target="tpu_custom_call" | custom-call | tf_op jit(solution)/shard_map/gram/pallas_call | solution.py:195
  20.4 9.7 %all-to-all-start = ((f32[32,24,128]{2,1,0:T(8,128)}), f32[32,24,128]{2,1,0:T(8,128)S(1)}, u32[]{:S(2)}, u32[]{:S(2)}) async-start(f32[32,24,128]{2,1,0:T(8,128)} %gram.1), calls=%async_computation | async-start | bytes 786432 | tf_op jit(solution)/shard_map/all_to_all | solution.py:261
  30.1 0.0 copy-start
  30.1 0.0 collective-permute-done.2
  30.1 2.1 %collective-permute-start.4 = (f32[96,512]{1,0:T(8,128)}, f32[96,512]{1,0:T(8,128)S(1)}, u32[]{:S(2)}, u32[]{:S(2)}) collective-permute-start(f32[96,512]{1,0:T(8,128)} %collective-permute-done.2), channel_id=1, source_target_pairs={{0,1},{1,2},{2,3},{3,4},{4,5},{5,6},{6,7},{7,0},{8,9},{9,10},{10,1... | collective-permute-start | bytes 589832 | tf_op jit(solution)/shard_map/ppermute | solution.py:253
  32.2 0.0 collective-permute-done.3
  32.2 4.6 %collective-permute-start.5 = (f32[96,512]{1,0:T(8,128)}, f32[96,512]{1,0:T(8,128)S(1)}, u32[]{:S(2)}, u32[]{:S(2)}) collective-permute-start(f32[96,512]{1,0:T(8,128)} %collective-permute-done.3), channel_id=1, source_target_pairs={{0,7},{1,0},{2,1},{3,2},{4,3},{5,4},{6,5},{7,6},{8,15},{9,8},{10,9... | collective-permute-start | bytes 589832 | tf_op jit(solution)/shard_map/ppermute | solution.py:256
  36.8 0.9 constant_dynamic-update-slice_fusion.6
  37.7 0.9 constant_dynamic-update-slice_fusion.5
  38.7 0.8 collective-permute-done.4
  39.5 1.9 %collective-permute-start.6 = (f32[96,512]{1,0:T(8,128)S(1)}, f32[96,512]{1,0:T(8,128)S(1)}, u32[]{:S(2)}, u32[]{:S(2)}) collective-permute-start(f32[96,512]{1,0:T(8,128)S(1)} %collective-permute-done.4), channel_id=1, source_target_pairs={{0,1},{1,2},{2,3},{3,4},{4,5},{5,6},{6,7},{7,0},{8,9},{9,10},{10,1... | collective-permute-start | bytes 589832 | tf_op jit(solution)/shard_map/ppermute | solution.py:253
  41.4 0.0 collective-permute-done.5
  41.4 4.6 %collective-permute-start.7 = (f32[96,512]{1,0:T(8,128)S(1)}, f32[96,512]{1,0:T(8,128)S(1)}, u32[]{:S(2)}, u32[]{:S(2)}) collective-permute-start(f32[96,512]{1,0:T(8,128)S(1)} %collective-permute-done.5), channel_id=1, source_target_pairs={{0,7},{1,0},{2,1},{3,2},{4,3},{5,4},{6,5},{7,6},{8,15},{9,8},{10,9... | collective-permute-start | bytes 589832 | tf_op jit(solution)/shard_map/ppermute | solution.py:256
  46.0 1.6 collective-permute-done.6
  47.6 1.9 %collective-permute-start.8 = (f32[96,512]{1,0:T(8,128)S(1)}, f32[96,512]{1,0:T(8,128)S(1)}, u32[]{:S(2)}, u32[]{:S(2)}) collective-permute-start(f32[96,512]{1,0:T(8,128)S(1)} %collective-permute-done.6), channel_id=1, source_target_pairs={{0,1},{1,2},{2,3},{3,4},{4,5},{5,6},{6,7},{7,0},{8,9},{9,10},{10,1... | collective-permute-start | bytes 589832 | tf_op jit(solution)/shard_map/ppermute | solution.py:253
  49.6 0.0 collective-permute-done.7
  49.6 5.6 %collective-permute-done.8 = f32[96,512]{1,0:T(8,128)S(1)} collective-permute-done((f32[96,512]{1,0:T(8,128)S(1)}, f32[96,512]{1,0:T(8,128)S(1)}, u32[]{:S(2)}, u32[]{:S(2)}) %collective-permute-start.8) | collective-permute-done | bytes 196640 | tf_op jit(solution)/shard_map/ppermute | solution.py:253
  55.3 1.6 fusion
  56.9 5.4 %collective-permute-start.9 = (f32[256,512]{1,0:T(8,128)}, f32[256,512]{1,0:T(8,128)}, u32[]{:S(2)}, u32[]{:S(2)}) collective-permute-start(f32[256,512]{1,0:T(8,128)} %fusion), channel_id=1, source_target_pairs={{0,8},{8,0},{1,9},{9,1},{2,10},{10,2},{3,11},{11,3},{4,12},{12,4},... | collective-permute-start | bytes 1572872 | tf_op jit(solution)/shard_map/ppermute | solution.py:270
  62.3 1.7 fusion.2
  64.0 0.0 all-to-all-done
  64.0 0.6 broadcast_in_dim.11
  64.7 3.7 %all-to-all-start.1 = ((f32[8,24,128]{2,1,0:T(8,128)}), f32[8,24,128]{2,1,0:T(8,128)S(1)}, u32[]{:S(2)}, u32[]{:S(2)}) async-start(f32[8,24,128]{2,1,0:T(8,128)} %broadcast_in_dim.11), calls=%async_computation.1 | async-start | bytes 196608 | tf_op jit(solution)/shard_map/all_to_all | solution.py:234
  68.4 2.1 %add_bitcast_fusion = f32[32,8,512]{2,1,0:T(8,128)} fusion(f32[256,512]{1,0:T(8,128)} %fusion.2, f32[256,512]{1,0:T(8,128)} %collective-permute-done.9), kind=kLoop, calls=%fused_computation.7 | loop fusion | flops 131072 | bytes 1572864 | tf_op jit(solution)/shard_map/reshape | solution.py:273
  70.4 5.8 %all-to-all-done.1 = f32[8,24,128]{2,1,0:T(8,128)S(1)} async-done(((f32[8,24,128]{2,1,0:T(8,128)}), f32[8,24,128]{2,1,0:T(8,128)S(1)}, u32[]{:S(2)}, u32[]{:S(2)}) %all-to-all-start.1) | async-done | bytes 98336 | tf_op jit(solution)/shard_map/all_to_all | solution.py:234
  76.2 9.4 %all-to-all-start.3 = ((f32[32,8,512]{2,1,0:T(8,128)}), f32[32,8,512]{2,1,0:T(8,128)}, u32[]{:S(2)}, u32[]{:S(2)}) async-start(f32[32,8,512]{2,1,0:T(8,128)} %add_bitcast_fusion), calls=%async_computation.3 | async-start | bytes 1048576 | tf_op jit(solution)/shard_map/all_to_all | solution.py:273
  85.6 13.5 %all-to-all-done.3 = f32[32,8,512]{2,1,0:T(8,128)} async-done(((f32[32,8,512]{2,1,0:T(8,128)}), f32[32,8,512]{2,1,0:T(8,128)}, u32[]{:S(2)}, u32[]{:S(2)}) %all-to-all-start.3) | async-done | bytes 524320 | tf_op jit(solution)/shard_map/all_to_all | solution.py:273
  99.2 0.8 broadcast_in_dim.12
  99.9 8.1 %all-to-all-start.2 = ((f32[32,24,128]{2,1,0:T(8,128)}), f32[32,24,128]{2,1,0:T(8,128)S(1)}, u32[]{:S(2)}, u32[]{:S(2)}) async-start(f32[32,24,128]{2,1,0:T(8,128)} %broadcast_in_dim.12), calls=%async_computation.2 | async-start | bytes 786432 | tf_op jit(solution)/shard_map/all_to_all | solution.py:234
  108.0 1.1 reduce_sum.29
  109.1 9.4 %all-to-all-done.2.mine_ref = f32[32,24,128]{2,1,0:T(8,128)S(1)} async-done(((f32[32,24,128]{2,1,0:T(8,128)}), f32[32,24,128]{2,1,0:T(8,128)S(1)}, u32[]{:S(2)}, u32[]{:S(2)}) %all-to-all-start.2) | async-done | bytes 393248 | tf_op jit(solution)/shard_map/all_to_all | solution.py:234
  118.5 0.9 broadcast_in_dim.28
  119.5 7.5 %all-to-all-start.4 = ((f32[32,8,512]{2,1,0:T(8,128)}), f32[32,8,512]{2,1,0:T(8,128)}, u32[]{:S(2)}, u32[]{:S(2)}) async-start(f32[32,8,512]{2,1,0:T(8,128)} %broadcast_in_dim.28), calls=%async_computation.4 | async-start | bytes 1048576 | tf_op jit(solution)/shard_map/all_to_all | solution.py:234
  127.0 4.6 %collective-permute-start.1 = (f32[32,24,128]{2,1,0:T(8,128)S(1)}, f32[32,24,128]{2,1,0:T(8,128)}, u32[]{:S(2)}, u32[]{:S(2)}) collective-permute-start(f32[32,24,128]{2,1,0:T(8,128)S(1)} %all-to-all-done.2.mine_ref), channel_id=1, source_target_pairs={{0,8},{8,0},{1,9},{9,1},{2,10},{10,2},{3,11},{11,3},{4,12},{12,4},... | collective-permute-start | bytes 1179656 | tf_op jit(solution)/shard_map/ppermute | solution.py:265
  131.6 8.0 %all-to-all-done.4 = f32[32,8,512]{2,1,0:T(8,128)} async-done(((f32[32,8,512]{2,1,0:T(8,128)}), f32[32,8,512]{2,1,0:T(8,128)}, u32[]{:S(2)}, u32[]{:S(2)}) %all-to-all-start.4) | async-done | bytes 524320 | tf_op jit(solution)/shard_map/all_to_all | solution.py:234
  139.6 6.9 %collective-permute-start.10 = (f32[256,512]{1,0:T(8,128)}, f32[256,512]{1,0:T(8,128)}, u32[]{:S(2)}, u32[]{:S(2)}) collective-permute-start(f32[256,512]{1,0:T(8,128)} %bitcast.2), channel_id=1, source_target_pairs={{0,8},{8,0},{1,9},{9,1},{2,10},{10,2},{3,11},{11,3},{4,12},{12,4},... | collective-permute-start | bytes 1572872 | tf_op jit(solution)/shard_map/ppermute | solution.py:276
  146.5 11.5 %factor_top.1 = (f32[256,512]{1,0:T(8,128)}, f32[256,256]{1,0:T(8,128)}, f32[256,512]{1,0:T(8,128)}, f32[8,512]{1,0:T(8,128)}) custom-call(s32[1]{0:T(128)} %bitcast.which, f32[32,24,128]{2,1,0:T(8,128)} %copy-done.1, f32[32,24,128]{2,1,0:T(8,128)} %collective-permute-done.1.other_ref), custom_call_target="tpu_custom_call" | custom-call | tf_op jit(solution)/shard_map/factor_top/pallas_call | solution.py:206
  158.0 12.3 %factor_low.1 = (f32[512,512]{1,0:T(8,128)}, f32[512,512]{1,0:T(8,128)}) custom-call(f32[256,512]{1,0:T(8,128)} %get-tuple-element.8.top_ref, f32[256,256]{1,0:T(8,128)} %get-tuple-element.9.mtop_ref, f32[256,512]{1,0:T(8,128)} %get-tuple-element.10.tail_ref, f32[8,512]{1,0:T(8,128)} %get-tuple-element.11.s_ref), custom_call_target="tpu_custom_call" | custom-call | tf_op jit(solution)/shard_map/factor_low/pallas_call | solution.py:218
  170.3 2.3 %fusion.5 = f32[512,512]{1,0:T(8,128)S(1)} fusion(f32[512,512]{1,0:T(8,128)} %get-tuple-element.13, s32[]{:T(128)S(6)} %select_n.78, f32[32,8,512]{2,1,0:T(8,128)} %all-to-all-done.4), kind=kOutput, calls=%fused_computation.8 | convolution fusion | flops 805306368 | bytes 2097156 | tf_op jit(solution)/shard_map/dot_general | solution.py:229
  172.6 2.1 %convolution_add_fusion = f32[512,512]{1,0:T(8,128)S(1)} fusion(f32[512,512]{1,0:T(8,128)S(1)} %fusion.5, f32[256,512]{1,0:T(8,128)} %collective-permute-done.10, f32[512,512]{1,0:T(8,128)S(1)} %copy-done.2, s32[]{:T(128)S(6)} %select_n.79), kind=kOutput, calls=%fused_computation.1 | convolution fusion | flops 805568512 | bytes 3145732 | tf_op jit(solution)/shard_map/dot_general | solution.py:229
  174.8 2.6 %convolution_subtract_fusion = f32[768,512]{1,0:T(8,128)} fusion(f32[768,512]{1,0:T(8,128)S(1)} %copy-done, f32[768,512]{1,0:T(8,128)S(1)} %constant_dynamic-update-slice_fusion, f32[512,512]{1,0:T(8,128)S(1)} %convolution_add_fusion), kind=kOutput, calls=%fused_computation | convolution fusion | flops 1208352768 | bytes 5767168 | tf_op jit(solution)/shard_map/dot_general | solution.py:229
  (18 shorter events, 0.2 us)
Async XLA Ops:
  0.6 16.5 %copy-start.3 = (f32[96,512]{1,0:T(8,128)S(1)}, f32[96,512]{1,0:T(8,128)}, u32[]{:S(2)}) copy-start(f32[96,512]{1,0:T(8,128)} %a_ref.1) | copy-start | bytes 589828
  0.6 16.5 %collective-permute-start = (f32[96,512]{1,0:T(8,128)}, f32[96,512]{1,0:T(8,128)S(1)}, u32[]{:S(2)}, u32[]{:S(2)}) collective-permute-start(f32[96,512]{1,0:T(8,128)} %a_ref.1), channel_id=1, source_target_pairs={{0,8},{8,0},{1,9},{9,1},{2,10},{10,2},{3,11},{11,3},{4,12},{12,4},... | collective-permute-start | bytes 589832 | tf_op jit(solution)/shard_map/ppermute | solution.py:259
  9.5 20.6 %collective-permute-start.2 = (f32[96,512]{1,0:T(8,128)}, f32[96,512]{1,0:T(8,128)}, u32[]{:S(2)}, u32[]{:S(2)}) collective-permute-start(f32[96,512]{1,0:T(8,128)} %a_ref.1), channel_id=1, source_target_pairs={{0,1},{1,2},{2,3},{3,4},{4,5},{5,6},{6,7},{7,0},{8,9},{9,10},{10,1... | collective-permute-start | bytes 589832 | tf_op jit(solution)/shard_map/ppermute | solution.py:253
  11.5 20.7 %collective-permute-start.3 = (f32[96,512]{1,0:T(8,128)}, f32[96,512]{1,0:T(8,128)}, u32[]{:S(2)}, u32[]{:S(2)}) collective-permute-start(f32[96,512]{1,0:T(8,128)} %a_ref.1), channel_id=1, source_target_pairs={{0,7},{1,0},{2,1},{3,2},{4,3},{5,4},{6,5},{7,6},{8,15},{9,8},{10,9... | collective-permute-start | bytes 589832 | tf_op jit(solution)/shard_map/ppermute | solution.py:256
  17.1 0.7 copy-start.4
  20.4 43.6 %all-to-all-start = ((f32[32,24,128]{2,1,0:T(8,128)}), f32[32,24,128]{2,1,0:T(8,128)S(1)}, u32[]{:S(2)}, u32[]{:S(2)}) async-start(f32[32,24,128]{2,1,0:T(8,128)} %gram.1), calls=%async_computation | async-start | bytes 786432 | tf_op jit(solution)/shard_map/all_to_all | solution.py:261
  30.1 25.2 %copy-start = (f32[768,512]{1,0:T(8,128)S(1)}, f32[768,512]{1,0:T(8,128)}, u32[]{:S(2)}) copy-start(f32[768,512]{1,0:T(8,128)} %param.3) | copy-start | bytes 4718596
  30.1 9.4 %collective-permute-start.4 = (f32[96,512]{1,0:T(8,128)}, f32[96,512]{1,0:T(8,128)S(1)}, u32[]{:S(2)}, u32[]{:S(2)}) collective-permute-start(f32[96,512]{1,0:T(8,128)} %collective-permute-done.2), channel_id=1, source_target_pairs={{0,1},{1,2},{2,3},{3,4},{4,5},{5,6},{6,7},{7,0},{8,9},{9,10},{10,1... | collective-permute-start | bytes 589832 | tf_op jit(solution)/shard_map/ppermute | solution.py:253
  32.2 9.2 %collective-permute-start.5 = (f32[96,512]{1,0:T(8,128)}, f32[96,512]{1,0:T(8,128)S(1)}, u32[]{:S(2)}, u32[]{:S(2)}) collective-permute-start(f32[96,512]{1,0:T(8,128)} %collective-permute-done.3), channel_id=1, source_target_pairs={{0,7},{1,0},{2,1},{3,2},{4,3},{5,4},{6,5},{7,6},{8,15},{9,8},{10,9... | collective-permute-start | bytes 589832 | tf_op jit(solution)/shard_map/ppermute | solution.py:256
  39.5 8.1 %collective-permute-start.6 = (f32[96,512]{1,0:T(8,128)S(1)}, f32[96,512]{1,0:T(8,128)S(1)}, u32[]{:S(2)}, u32[]{:S(2)}) collective-permute-start(f32[96,512]{1,0:T(8,128)S(1)} %collective-permute-done.4), channel_id=1, source_target_pairs={{0,1},{1,2},{2,3},{3,4},{4,5},{5,6},{6,7},{7,0},{8,9},{9,10},{10,1... | collective-permute-start | bytes 589832 | tf_op jit(solution)/shard_map/ppermute | solution.py:253
  41.4 8.2 %collective-permute-start.7 = (f32[96,512]{1,0:T(8,128)S(1)}, f32[96,512]{1,0:T(8,128)S(1)}, u32[]{:S(2)}, u32[]{:S(2)}) collective-permute-start(f32[96,512]{1,0:T(8,128)S(1)} %collective-permute-done.5), channel_id=1, source_target_pairs={{0,7},{1,0},{2,1},{3,2},{4,3},{5,4},{6,5},{7,6},{8,15},{9,8},{10,9... | collective-permute-start | bytes 589832 | tf_op jit(solution)/shard_map/ppermute | solution.py:256
  47.6 7.6 %collective-permute-start.8 = (f32[96,512]{1,0:T(8,128)S(1)}, f32[96,512]{1,0:T(8,128)S(1)}, u32[]{:S(2)}, u32[]{:S(2)}) collective-permute-start(f32[96,512]{1,0:T(8,128)S(1)} %collective-permute-done.6), channel_id=1, source_target_pairs={{0,1},{1,2},{2,3},{3,4},{4,5},{5,6},{6,7},{7,0},{8,9},{9,10},{10,1... | collective-permute-start | bytes 589832 | tf_op jit(solution)/shard_map/ppermute | solution.py:253
  56.9 11.4 %collective-permute-start.9 = (f32[256,512]{1,0:T(8,128)}, f32[256,512]{1,0:T(8,128)}, u32[]{:S(2)}, u32[]{:S(2)}) collective-permute-start(f32[256,512]{1,0:T(8,128)} %fusion), channel_id=1, source_target_pairs={{0,8},{8,0},{1,9},{9,1},{2,10},{10,2},{3,11},{11,3},{4,12},{12,4},... | collective-permute-start | bytes 1572872 | tf_op jit(solution)/shard_map/ppermute | solution.py:270
  64.7 11.5 %all-to-all-start.1 = ((f32[8,24,128]{2,1,0:T(8,128)}), f32[8,24,128]{2,1,0:T(8,128)S(1)}, u32[]{:S(2)}, u32[]{:S(2)}) async-start(f32[8,24,128]{2,1,0:T(8,128)} %broadcast_in_dim.11), calls=%async_computation.1 | async-start | bytes 196608 | tf_op jit(solution)/shard_map/all_to_all | solution.py:234
  76.2 22.9 %all-to-all-start.3 = ((f32[32,8,512]{2,1,0:T(8,128)}), f32[32,8,512]{2,1,0:T(8,128)}, u32[]{:S(2)}, u32[]{:S(2)}) async-start(f32[32,8,512]{2,1,0:T(8,128)} %add_bitcast_fusion), calls=%async_computation.3 | async-start | bytes 1048576 | tf_op jit(solution)/shard_map/all_to_all | solution.py:273
  99.9 18.6 %all-to-all-start.2 = ((f32[32,24,128]{2,1,0:T(8,128)}), f32[32,24,128]{2,1,0:T(8,128)S(1)}, u32[]{:S(2)}, u32[]{:S(2)}) async-start(f32[32,24,128]{2,1,0:T(8,128)} %broadcast_in_dim.12), calls=%async_computation.2 | async-start | bytes 786432 | tf_op jit(solution)/shard_map/all_to_all | solution.py:234
  118.5 28.0 %copy-start.1 = (f32[32,24,128]{2,1,0:T(8,128)}, f32[32,24,128]{2,1,0:T(8,128)S(1)}, u32[]{:S(2)}) copy-start(f32[32,24,128]{2,1,0:T(8,128)S(1)} %all-to-all-done.2.mine_ref) | copy-start | bytes 1179652
  119.5 20.1 %all-to-all-start.4 = ((f32[32,8,512]{2,1,0:T(8,128)}), f32[32,8,512]{2,1,0:T(8,128)}, u32[]{:S(2)}, u32[]{:S(2)}) async-start(f32[32,8,512]{2,1,0:T(8,128)} %broadcast_in_dim.28), calls=%async_computation.4 | async-start | bytes 1048576 | tf_op jit(solution)/shard_map/all_to_all | solution.py:234
  127.0 19.5 %collective-permute-start.1 = (f32[32,24,128]{2,1,0:T(8,128)S(1)}, f32[32,24,128]{2,1,0:T(8,128)}, u32[]{:S(2)}, u32[]{:S(2)}) collective-permute-start(f32[32,24,128]{2,1,0:T(8,128)S(1)} %all-to-all-done.2.mine_ref), channel_id=1, source_target_pairs={{0,8},{8,0},{1,9},{9,1},{2,10},{10,2},{3,11},{11,3},{4,12},{12,4},... | collective-permute-start | bytes 1179656 | tf_op jit(solution)/shard_map/ppermute | solution.py:265
  139.6 33.0 %collective-permute-start.10 = (f32[256,512]{1,0:T(8,128)}, f32[256,512]{1,0:T(8,128)}, u32[]{:S(2)}, u32[]{:S(2)}) collective-permute-start(f32[256,512]{1,0:T(8,128)} %bitcast.2), channel_id=1, source_target_pairs={{0,8},{8,0},{1,9},{9,1},{2,10},{10,2},{3,11},{11,3},{4,12},{12,4},... | collective-permute-start | bytes 1572872 | tf_op jit(solution)/shard_map/ppermute | solution.py:276
  170.3 2.3 %copy-start.2 = (f32[512,512]{1,0:T(8,128)S(1)}, f32[512,512]{1,0:T(8,128)}, u32[]{:S(2)}) copy-start(f32[512,512]{1,0:T(8,128)} %get-tuple-element.13) | copy-start | bytes 3145732

commit v3 on v2

--- a/solution.py
+++ b/solution.py
@@ -163,7 +163,7 @@
     tail_out[...] = aug[h:B, h:]
 
 
-def low_kernel(top_ref, mtop_ref, tail_ref, s_ref, r_out, g_out, aug, inv, low):
+def low_kernel(which, top_ref, mtop_ref, tail_ref, s_ref, r_out, g_out, aug, inv, low):
     h = B // 2
     r_out[0:h, :] = top_ref[...]
     r_out[h:B, 0:h] = jnp.zeros((h, h), F32)
@@ -182,9 +182,11 @@
     def square(a, b):
         return lax.dot_general(a, b, (((0,), (0,)), ((), ())), precision=HI, preferred_element_type=F32)
 
-    g_out[0:h, 0:h] = square(low[:, 0:h], low[:, 0:h]) + square(mtop_ref[...], mtop_ref[...])
-    g_out[h:B, :] = square(low[:, h:B], low[...])
-    g_out[0:h, h:B] = square(low[:, 0:h], low[:, h:B])
+    upper = pl.ds(pl.multiple_of(which[0] * h, h), h)
+    lower = pl.ds(pl.multiple_of((1 - which[0]) * h, h), h)
+    g_out[upper, 0:h] = square(low[:, 0:h], low[:, 0:h]) + square(mtop_ref[...], mtop_ref[...])
+    g_out[upper, h:B] = square(low[:, 0:h], low[:, h:B])
+    g_out[lower, :] = square(low[:, h:B], low[...])
 
 
 VM = pl.BlockSpec(memory_space=pltpu.VMEM)
@@ -213,16 +215,16 @@
     )(which, mine, other)
 
 
-def factor_low(top, top_inverse, tail, scales):
+def factor_low(which, top, top_inverse, tail, scales):
     h = B // 2
     return pl.pallas_call(
         low_kernel,
         out_shape=[jax.ShapeDtypeStruct((B, B), F32)] * 2,
-        in_specs=[VM] * 4,
+        in_specs=[SM] + [VM] * 4,
         out_specs=[VM] * 2,
         scratch_shapes=[pltpu.VMEM((h, h + B), F32), pltpu.VMEM((2 * NB, NB), F32), pltpu.VMEM((h, B), F32)],
         name="factor_low",
-    )(top, top_inverse, tail, scales)
+    )(which, top, top_inverse, tail, scales)
 
 
 def dot(a, b, dims, precision=HI):
@@ -264,7 +266,7 @@
     mine = spread(own, plane, ring).reshape(half.shape)
     other = lax.ppermute(mine, "c", swap)
     top, top_inverse, tail, scales = factor_top(which, mine, other, total_rows)
-    upper, ginv = factor_low(top, top_inverse, tail, scales)
+    upper, ginv = factor_low(which, top, top_inverse, tail, scales)
 
     give = dot(lax.dynamic_slice(block, (0, (1 - core) * h), (depth * each, h)), trailing, ((0,), (0,)), high)
     got = lax.ppermute(give, "c", swap)
@@ -275,8 +277,8 @@
     near = spread(own, plane, ring).reshape(h, -1)
     far = lax.ppermute(near, "c", swap)
 
-    weights = dot(lax.dynamic_slice(ginv, (core * h, 0), (h, B)), near, ((0,), (0,)))
-    weights = weights + dot(lax.dynamic_slice(ginv, ((1 - core) * h, 0), (h, B)), far, ((0,), (0,)))
+    weights = dot(ginv[:h], near, ((0,), (0,)))
+    weights = weights + dot(ginv[h:], far, ((0,), (0,)))
     residual = trailing - dot(block, weights, ((1,), (0,)), high)
     return (upper, residual)
 

time: 179 us -> 179 us (level)
  no operation moved by 1% of the time
where the time goes in v3:
time: 179 us; the launch traced here: 177 us
  starting transfers between devices  86.3 us (48%)
  waiting for transfers between devices  44.8 us (25%)
  Pallas kernels  26.4 us (15%)
  matrix products  10.3 us (6%)
  local copies, waits for them, and re-layouts  5.22 us (3%)
  other arithmetic  3.22 us (2%)
    all_to_all x3, waiting for transfers between devices, spread(): return lax.all_to_all(copies, axes, 0, 0, tiled=True)  23.2 us
    all_to_all x3, starting transfers between devices, spread(): return lax.all_to_all(copies, axes, 0, 0, tiled=True)  19.3 us
    ppermute x3, starting transfers between devices, per_device(): back = lax.ppermute(back, 'z', [(i, (i - 1) % depth) for i in range(depth)])  14.5 us
    all_to_all x1, waiting for transfers between devices, per_device(): lax.all_to_all((keep + got).reshape(ring, h // ring, -1), plane, 0, 0, ti...  13.5 us
    pallas_call x1, Pallas kernels, factor_low(): pl.pallas_call(low_kernel, out_shape=[jax.ShapeDtypeStruct((B, B), F32)]...  12.3 us
    pallas_call x1, Pallas kernels, factor_top(): pl.pallas_call(functools.partial(top_kernel, 1.0 / math.sqrt(total_rows))...  11.5 us
    dot_general x5, matrix products, dot(): lax.dot_general(a, b, (dims, ((), ())), precision=precision, preferred_el...  10.3 us
    all_to_all x1, starting transfers between devices, per_device(): pieces = lax.all_to_all(half.reshape(ring, -1, NB), plane, 0, 0, tiled=True)  9.67 us
  transfers between devices with their start and end apart: 16, of which 7 were waited for; matrix products, arithmetic and copies ran while one was open for 7% of the time, Pallas kernels for 15%

profile of v3, /device:TPU:1, one launch (start us, length us, event | category | flops | bytes accessed | tf_op | source)
XLA Modules:
  0.0 177.3 jit_solution(9257179965409509477)
XLA Ops:
  0.6 0.0 copy-start.3
  0.6 8.9 %collective-permute-start = (f32[96,512]{1,0:T(8,128)}, f32[96,512]{1,0:T(8,128)S(1)}, u32[]{:S(2)}, u32[]{:S(2)}) collective-permute-start(f32[96,512]{1,0:T(8,128)} %a_ref.1), channel_id=1, source_target_pairs={{0,8},{8,0},{1,9},{9,1},{2,10},{10,2},{3,11},{11,3},{4,12},{12,4},... | collective-permute-start | bytes 589832 | tf_op jit(solution)/shard_map/ppermute | solution.py:261
  9.5 1.9 %collective-permute-start.2 = (f32[96,512]{1,0:T(8,128)}, f32[96,512]{1,0:T(8,128)}, u32[]{:S(2)}, u32[]{:S(2)}) collective-permute-start(f32[96,512]{1,0:T(8,128)} %a_ref.1), channel_id=1, source_target_pairs={{0,1},{1,2},{2,3},{3,4},{4,5},{5,6},{6,7},{7,0},{8,9},{9,10},{10,1... | collective-permute-start | bytes 589832 | tf_op jit(solution)/shard_map/ppermute | solution.py:255
  11.5 5.3 %collective-permute-start.3 = (f32[96,512]{1,0:T(8,128)}, f32[96,512]{1,0:T(8,128)}, u32[]{:S(2)}, u32[]{:S(2)}) collective-permute-start(f32[96,512]{1,0:T(8,128)} %a_ref.1), channel_id=1, source_target_pairs={{0,7},{1,0},{2,1},{3,2},{4,3},{5,4},{6,5},{7,6},{8,15},{9,8},{10,9... | collective-permute-start | bytes 589832 | tf_op jit(solution)/shard_map/ppermute | solution.py:258
  16.9 0.2 broadcast_in_dim.13
  17.1 0.0 copy-start.4
  17.2 0.7 copy-done.4
  17.8 2.6 %gram.1 = f32[32,24,128]{2,1,0:T(8,128)} custom-call(s32[1]{0:T(128)} %bitcast.which, f32[96,512]{1,0:T(8,128)} %a_ref.1, f32[96,512]{1,0:T(8,128)} %copy-done.4), custom_call_target="tpu_custom_call" | custom-call | tf_op jit(solution)/shard_map/gram/pallas_call | solution.py:197
  20.4 9.7 %all-to-all-start = ((f32[32,24,128]{2,1,0:T(8,128)}), f32[32,24,128]{2,1,0:T(8,128)S(1)}, u32[]{:S(2)}, u32[]{:S(2)}) async-start(f32[32,24,128]{2,1,0:T(8,128)} %gram.1), calls=%async_computation | async-start | bytes 786432 | tf_op jit(solution)/shard_map/all_to_all | solution.py:263
  30.1 0.0 copy-start
  30.1 0.0 collective-permute-done.2
  30.1 2.1 %collective-permute-start.4 = (f32[96,512]{1,0:T(8,128)}, f32[96,512]{1,0:T(8,128)S(1)}, u32[]{:S(2)}, u32[]{:S(2)}) collective-permute-start(f32[96,512]{1,0:T(8,128)} %collective-permute-done.2), channel_id=1, source_target_pairs={{0,1},{1,2},{2,3},{3,4},{4,5},{5,6},{6,7},{7,0},{8,9},{9,10},{10,1... | collective-permute-start | bytes 589832 | tf_op jit(solution)/shard_map/ppermute | solution.py:255
  32.2 0.0 collective-permute-done.3
  32.2 4.6 %collective-permute-start.5 = (f32[96,512]{1,0:T(8,128)}, f32[96,512]{1,0:T(8,128)S(1)}, u32[]{:S(2)}, u32[]{:S(2)}) collective-permute-start(f32[96,512]{1,0:T(8,128)} %collective-permute-done.3), channel_id=1, source_target_pairs={{0,7},{1,0},{2,1},{3,2},{4,3},{5,4},{6,5},{7,6},{8,15},{9,8},{10,9... | collective-permute-start | bytes 589832 | tf_op jit(solution)/shard_map/ppermute | solution.py:258
  36.8 0.9 constant_dynamic-update-slice_fusion.6
  37.7 0.9 constant_dynamic-update-slice_fusion.5
  38.7 0.8 collective-permute-done.4
  39.5 1.9 %collective-permute-start.6 = (f32[96,512]{1,0:T(8,128)S(1)}, f32[96,512]{1,0:T(8,128)S(1)}, u32[]{:S(2)}, u32[]{:S(2)}) collective-permute-start(f32[96,512]{1,0:T(8,128)S(1)} %collective-permute-done.4), channel_id=1, source_target_pairs={{0,1},{1,2},{2,3},{3,4},{4,5},{5,6},{6,7},{7,0},{8,9},{9,10},{10,1... | collective-permute-start | bytes 589832 | tf_op jit(solution)/shard_map/ppermute | solution.py:255
  41.4 0.0 collective-permute-done.5
  41.4 4.6 %collective-permute-start.7 = (f32[96,512]{1,0:T(8,128)S(1)}, f32[96,512]{1,0:T(8,128)S(1)}, u32[]{:S(2)}, u32[]{:S(2)}) collective-permute-start(f32[96,512]{1,0:T(8,128)S(1)} %collective-permute-done.5), channel_id=1, source_target_pairs={{0,7},{1,0},{2,1},{3,2},{4,3},{5,4},{6,5},{7,6},{8,15},{9,8},{10,9... | collective-permute-start | bytes 589832 | tf_op jit(solution)/shard_map/ppermute | solution.py:258
  46.0 1.6 collective-permute-done.6
  47.6 1.9 %collective-permute-start.8 = (f32[96,512]{1,0:T(8,128)S(1)}, f32[96,512]{1,0:T(8,128)S(1)}, u32[]{:S(2)}, u32[]{:S(2)}) collective-permute-start(f32[96,512]{1,0:T(8,128)S(1)} %collective-permute-done.6), channel_id=1, source_target_pairs={{0,1},{1,2},{2,3},{3,4},{4,5},{5,6},{6,7},{7,0},{8,9},{9,10},{10,1... | collective-permute-start | bytes 589832 | tf_op jit(solution)/shard_map/ppermute | solution.py:255
  49.6 0.0 collective-permute-done.7
  49.6 5.6 %collective-permute-done.8 = f32[96,512]{1,0:T(8,128)S(1)} collective-permute-done((f32[96,512]{1,0:T(8,128)S(1)}, f32[96,512]{1,0:T(8,128)S(1)}, u32[]{:S(2)}, u32[]{:S(2)}) %collective-permute-start.8) | collective-permute-done | bytes 196640 | tf_op jit(solution)/shard_map/ppermute | solution.py:255
  55.3 1.6 fusion
  56.9 5.4 %collective-permute-start.9 = (f32[256,512]{1,0:T(8,128)}, f32[256,512]{1,0:T(8,128)}, u32[]{:S(2)}, u32[]{:S(2)}) collective-permute-start(f32[256,512]{1,0:T(8,128)} %fusion), channel_id=1, source_target_pairs={{0,8},{8,0},{1,9},{9,1},{2,10},{10,2},{3,11},{11,3},{4,12},{12,4},... | collective-permute-start | bytes 1572872 | tf_op jit(solution)/shard_map/ppermute | solution.py:272
  62.3 1.7 fusion.2
  64.0 0.6 broadcast_in_dim.11
  64.7 3.7 %all-to-all-start.1 = ((f32[8,24,128]{2,1,0:T(8,128)}), f32[8,24,128]{2,1,0:T(8,128)S(1)}, u32[]{:S(2)}, u32[]{:S(2)}) async-start(f32[8,24,128]{2,1,0:T(8,128)} %broadcast_in_dim.11), calls=%async_computation.1 | async-start | bytes 196608 | tf_op jit(solution)/shard_map/all_to_all | solution.py:236
  68.4 0.0 collective-permute-done.9
  68.4 2.1 %add_bitcast_fusion = f32[32,8,512]{2,1,0:T(8,128)} fusion(f32[256,512]{1,0:T(8,128)} %fusion.2, f32[256,512]{1,0:T(8,128)} %collective-permute-done.9), kind=kLoop, calls=%fused_computation.7 | loop fusion | flops 131072 | bytes 1572864 | tf_op jit(solution)/shard_map/reshape | solution.py:275
  70.4 5.8 %all-to-all-done.1 = f32[8,24,128]{2,1,0:T(8,128)S(1)} async-done(((f32[8,24,128]{2,1,0:T(8,128)}), f32[8,24,128]{2,1,0:T(8,128)S(1)}, u32[]{:S(2)}, u32[]{:S(2)}) %all-to-all-start.1) | async-done | bytes 98336 | tf_op jit(solution)/shard_map/all_to_all | solution.py:236
  76.2 9.3 %all-to-all-start.3 = ((f32[32,8,512]{2,1,0:T(8,128)}), f32[32,8,512]{2,1,0:T(8,128)}, u32[]{:S(2)}, u32[]{:S(2)}) async-start(f32[32,8,512]{2,1,0:T(8,128)} %add_bitcast_fusion), calls=%async_computation.3 | async-start | bytes 1048576 | tf_op jit(solution)/shard_map/all_to_all | solution.py:275
  85.6 13.5 %all-to-all-done.3 = f32[32,8,512]{2,1,0:T(8,128)} async-done(((f32[32,8,512]{2,1,0:T(8,128)}), f32[32,8,512]{2,1,0:T(8,128)}, u32[]{:S(2)}, u32[]{:S(2)}) %all-to-all-start.3) | async-done | bytes 524320 | tf_op jit(solution)/shard_map/all_to_all | solution.py:275
  99.2 0.8 broadcast_in_dim.12
  99.9 8.1 %all-to-all-start.2 = ((f32[32,24,128]{2,1,0:T(8,128)}), f32[32,24,128]{2,1,0:T(8,128)S(1)}, u32[]{:S(2)}, u32[]{:S(2)}) async-start(f32[32,24,128]{2,1,0:T(8,128)} %broadcast_in_dim.12), calls=%async_computation.2 | async-start | bytes 786432 | tf_op jit(solution)/shard_map/all_to_all | solution.py:236
  108.0 1.1 reduce_sum.29
  109.1 9.4 %all-to-all-done.2.mine_ref = f32[32,24,128]{2,1,0:T(8,128)S(1)} async-done(((f32[32,24,128]{2,1,0:T(8,128)}), f32[32,24,128]{2,1,0:T(8,128)S(1)}, u32[]{:S(2)}, u32[]{:S(2)}) %all-to-all-start.2) | async-done | bytes 393248 | tf_op jit(solution)/shard_map/all_to_all | solution.py:236
  118.5 0.9 broadcast_in_dim.28
  119.5 7.5 %all-to-all-start.4 = ((f32[32,8,512]{2,1,0:T(8,128)}), f32[32,8,512]{2,1,0:T(8,128)}, u32[]{:S(2)}, u32[]{:S(2)}) async-start(f32[32,8,512]{2,1,0:T(8,128)} %broadcast_in_dim.28), calls=%async_computation.4 | async-start | bytes 1048576 | tf_op jit(solution)/shard_map/all_to_all | solution.py:236
  127.0 4.6 %collective-permute-start.1 = (f32[32,24,128]{2,1,0:T(8,128)S(1)}, f32[32,24,128]{2,1,0:T(8,128)}, u32[]{:S(2)}, u32[]{:S(2)}) collective-permute-start(f32[32,24,128]{2,1,0:T(8,128)S(1)} %all-to-all-done.2.mine_ref), channel_id=1, source_target_pairs={{0,8},{8,0},{1,9},{9,1},{2,10},{10,2},{3,11},{11,3},{4,12},{12,4},... | collective-permute-start | bytes 1179656 | tf_op jit(solution)/shard_map/ppermute | solution.py:267
  131.6 8.0 %all-to-all-done.4 = f32[32,8,512]{2,1,0:T(8,128)} async-done(((f32[32,8,512]{2,1,0:T(8,128)}), f32[32,8,512]{2,1,0:T(8,128)}, u32[]{:S(2)}, u32[]{:S(2)}) %all-to-all-start.4) | async-done | bytes 524320 | tf_op jit(solution)/shard_map/all_to_all | solution.py:236
  139.6 6.9 %collective-permute-start.10 = (f32[256,512]{1,0:T(8,128)}, f32[256,512]{1,0:T(8,128)}, u32[]{:S(2)}, u32[]{:S(2)}) collective-permute-start(f32[256,512]{1,0:T(8,128)} %bitcast.2), channel_id=1, source_target_pairs={{0,8},{8,0},{1,9},{9,1},{2,10},{10,2},{3,11},{11,3},{4,12},{12,4},... | collective-permute-start | bytes 1572872 | tf_op jit(solution)/shard_map/ppermute | solution.py:278
  146.5 11.5 %factor_top.1 = (f32[256,512]{1,0:T(8,128)}, f32[256,256]{1,0:T(8,128)}, f32[256,512]{1,0:T(8,128)}, f32[8,512]{1,0:T(8,128)}) custom-call(s32[1]{0:T(128)} %bitcast.which, f32[32,24,128]{2,1,0:T(8,128)} %copy-done.1, f32[32,24,128]{2,1,0:T(8,128)} %collective-permute-done.1.other_ref), custom_call_target="tpu_custom_call" | custom-call | tf_op jit(solution)/shard_map/factor_top/pallas_call | solution.py:208
  158.0 12.3 %factor_low.1 = (f32[512,512]{1,0:T(8,128)}, f32[512,512]{1,0:T(8,128)}) custom-call(s32[1]{0:T(128)} %bitcast.which, f32[256,512]{1,0:T(8,128)} %get-tuple-element.8.top_ref, f32[256,256]{1,0:T(8,128)} %get-tuple-element.9.mtop_ref, f32[256,512]{1,0:T(8,128)} %get-tuple-element.10.tail_ref, f32[8,512]{1,0:T(8,128)} %get-tuple-element.11.s_ref), custom_call_target="tpu_custom_call" | custom-call | tf_op jit(solution)/shard_map/factor_low/pallas_call | solution.py:220
  170.3 2.3 %fusion.5 = f32[512,512]{1,0:T(8,128)S(1)} fusion(f32[512,512]{1,0:T(8,128)} %get-tuple-element.13, f32[32,8,512]{2,1,0:T(8,128)} %all-to-all-done.4), kind=kOutput, calls=%fused_computation.8 | convolution fusion | flops 805306368 | bytes 2097152 | tf_op jit(solution)/shard_map/dot_general | solution.py:231
  172.6 2.1 %convolution_add_fusion = f32[512,512]{1,0:T(8,128)S(1)} fusion(f32[512,512]{1,0:T(8,128)S(1)} %fusion.5, f32[256,512]{1,0:T(8,128)} %collective-permute-done.10, f32[512,512]{1,0:T(8,128)S(1)} %copy-done.2), kind=kOutput, calls=%fused_computation.1 | convolution fusion | flops 805568512 | bytes 3145728 | tf_op jit(solution)/shard_map/dot_general | solution.py:231
  174.7 2.6 %convolution_subtract_fusion = f32[768,512]{1,0:T(8,128)} fusion(f32[768,512]{1,0:T(8,128)S(1)} %copy-done, f32[768,512]{1,0:T(8,128)S(1)} %constant_dynamic-update-slice_fusion, f32[512,512]{1,0:T(8,128)S(1)} %convolution_add_fusion), kind=kOutput, calls=%fused_computation | convolution fusion | flops 1208352768 | bytes 5767168 | tf_op jit(solution)/shard_map/dot_general | solution.py:231
  (18 shorter events, 0.2 us)
Async XLA Ops:
  0.6 16.5 %copy-start.3 = (f32[96,512]{1,0:T(8,128)S(1)}, f32[96,512]{1,0:T(8,128)}, u32[]{:S(2)}) copy-start(f32[96,512]{1,0:T(8,128)} %a_ref.1) | copy-start | bytes 589828
  0.6 16.5 %collective-permute-start = (f32[96,512]{1,0:T(8,128)}, f32[96,512]{1,0:T(8,128)S(1)}, u32[]{:S(2)}, u32[]{:S(2)}) collective-permute-start(f32[96,512]{1,0:T(8,128)} %a_ref.1), channel_id=1, source_target_pairs={{0,8},{8,0},{1,9},{9,1},{2,10},{10,2},{3,11},{11,3},{4,12},{12,4},... | collective-permute-start | bytes 589832 | tf_op jit(solution)/shard_map/ppermute | solution.py:261
  9.5 20.6 %collective-permute-start.2 = (f32[96,512]{1,0:T(8,128)}, f32[96,512]{1,0:T(8,128)}, u32[]{:S(2)}, u32[]{:S(2)}) collective-permute-start(f32[96,512]{1,0:T(8,128)} %a_ref.1), channel_id=1, source_target_pairs={{0,1},{1,2},{2,3},{3,4},{4,5},{5,6},{6,7},{7,0},{8,9},{9,10},{10,1... | collective-permute-start | bytes 589832 | tf_op jit(solution)/shard_map/ppermute | solution.py:255
  11.5 20.7 %collective-permute-start.3 = (f32[96,512]{1,0:T(8,128)}, f32[96,512]{1,0:T(8,128)}, u32[]{:S(2)}, u32[]{:S(2)}) collective-permute-start(f32[96,512]{1,0:T(8,128)} %a_ref.1), channel_id=1, source_target_pairs={{0,7},{1,0},{2,1},{3,2},{4,3},{5,4},{6,5},{7,6},{8,15},{9,8},{10,9... | collective-permute-start | bytes 589832 | tf_op jit(solution)/shard_map/ppermute | solution.py:258
  17.1 0.7 copy-start.4
  20.4 43.6 %all-to-all-start = ((f32[32,24,128]{2,1,0:T(8,128)}), f32[32,24,128]{2,1,0:T(8,128)S(1)}, u32[]{:S(2)}, u32[]{:S(2)}) async-start(f32[32,24,128]{2,1,0:T(8,128)} %gram.1), calls=%async_computation | async-start | bytes 786432 | tf_op jit(solution)/shard_map/all_to_all | solution.py:263
  30.1 25.2 %copy-start = (f32[768,512]{1,0:T(8,128)S(1)}, f32[768,512]{1,0:T(8,128)}, u32[]{:S(2)}) copy-start(f32[768,512]{1,0:T(8,128)} %param.3) | copy-start | bytes 4718596
  30.1 9.4 %collective-permute-start.4 = (f32[96,512]{1,0:T(8,128)}, f32[96,512]{1,0:T(8,128)S(1)}, u32[]{:S(2)}, u32[]{:S(2)}) collective-permute-start(f32[96,512]{1,0:T(8,128)} %collective-permute-done.2), channel_id=1, source_target_pairs={{0,1},{1,2},{2,3},{3,4},{4,5},{5,6},{6,7},{7,0},{8,9},{9,10},{10,1... | collective-permute-start | bytes 589832 | tf_op jit(solution)/shard_map/ppermute | solution.py:255
  32.2 9.2 %collective-permute-start.5 = (f32[96,512]{1,0:T(8,128)}, f32[96,512]{1,0:T(8,128)S(1)}, u32[]{:S(2)}, u32[]{:S(2)}) collective-permute-start(f32[96,512]{1,0:T(8,128)} %collective-permute-done.3), channel_id=1, source_target_pairs={{0,7},{1,0},{2,1},{3,2},{4,3},{5,4},{6,5},{7,6},{8,15},{9,8},{10,9... | collective-permute-start | bytes 589832 | tf_op jit(solution)/shard_map/ppermute | solution.py:258
  39.5 8.1 %collective-permute-start.6 = (f32[96,512]{1,0:T(8,128)S(1)}, f32[96,512]{1,0:T(8,128)S(1)}, u32[]{:S(2)}, u32[]{:S(2)}) collective-permute-start(f32[96,512]{1,0:T(8,128)S(1)} %collective-permute-done.4), channel_id=1, source_target_pairs={{0,1},{1,2},{2,3},{3,4},{4,5},{5,6},{6,7},{7,0},{8,9},{9,10},{10,1... | collective-permute-start | bytes 589832 | tf_op jit(solution)/shard_map/ppermute | solution.py:255
  41.4 8.2 %collective-permute-start.7 = (f32[96,512]{1,0:T(8,128)S(1)}, f32[96,512]{1,0:T(8,128)S(1)}, u32[]{:S(2)}, u32[]{:S(2)}) collective-permute-start(f32[96,512]{1,0:T(8,128)S(1)} %collective-permute-done.5), channel_id=1, source_target_pairs={{0,7},{1,0},{2,1},{3,2},{4,3},{5,4},{6,5},{7,6},{8,15},{9,8},{10,9... | collective-permute-start | bytes 589832 | tf_op jit(solution)/shard_map/ppermute | solution.py:258
  47.6 7.6 %collective-permute-start.8 = (f32[96,512]{1,0:T(8,128)S(1)}, f32[96,512]{1,0:T(8,128)S(1)}, u32[]{:S(2)}, u32[]{:S(2)}) collective-permute-start(f32[96,512]{1,0:T(8,128)S(1)} %collective-permute-done.6), channel_id=1, source_target_pairs={{0,1},{1,2},{2,3},{3,4},{4,5},{5,6},{6,7},{7,0},{8,9},{9,10},{10,1... | collective-permute-start | bytes 589832 | tf_op jit(solution)/shard_map/ppermute | solution.py:255
  56.9 11.5 %collective-permute-start.9 = (f32[256,512]{1,0:T(8,128)}, f32[256,512]{1,0:T(8,128)}, u32[]{:S(2)}, u32[]{:S(2)}) collective-permute-start(f32[256,512]{1,0:T(8,128)} %fusion), channel_id=1, source_target_pairs={{0,8},{8,0},{1,9},{9,1},{2,10},{10,2},{3,11},{11,3},{4,12},{12,4},... | collective-permute-start | bytes 1572872 | tf_op jit(solution)/shard_map/ppermute | solution.py:272
  64.7 11.6 %all-to-all-start.1 = ((f32[8,24,128]{2,1,0:T(8,128)}), f32[8,24,128]{2,1,0:T(8,128)S(1)}, u32[]{:S(2)}, u32[]{:S(2)}) async-start(f32[8,24,128]{2,1,0:T(8,128)} %broadcast_in_dim.11), calls=%async_computation.1 | async-start | bytes 196608 | tf_op jit(solution)/shard_map/all_to_all | solution.py:236
  76.2 22.9 %all-to-all-start.3 = ((f32[32,8,512]{2,1,0:T(8,128)}), f32[32,8,512]{2,1,0:T(8,128)}, u32[]{:S(2)}, u32[]{:S(2)}) async-start(f32[32,8,512]{2,1,0:T(8,128)} %add_bitcast_fusion), calls=%async_computation.3 | async-start | bytes 1048576 | tf_op jit(solution)/shard_map/all_to_all | solution.py:275
  99.9 18.6 %all-to-all-start.2 = ((f32[32,24,128]{2,1,0:T(8,128)}), f32[32,24,128]{2,1,0:T(8,128)S(1)}, u32[]{:S(2)}, u32[]{:S(2)}) async-start(f32[32,24,128]{2,1,0:T(8,128)} %broadcast_in_dim.12), calls=%async_computation.2 | async-start | bytes 786432 | tf_op jit(solution)/shard_map/all_to_all | solution.py:236
  118.5 28.0 %copy-start.1 = (f32[32,24,128]{2,1,0:T(8,128)}, f32[32,24,128]{2,1,0:T(8,128)S(1)}, u32[]{:S(2)}) copy-start(f32[32,24,128]{2,1,0:T(8,128)S(1)} %all-to-all-done.2.mine_ref) | copy-start | bytes 1179652
  119.5 20.1 %all-to-all-start.4 = ((f32[32,8,512]{2,1,0:T(8,128)}), f32[32,8,512]{2,1,0:T(8,128)}, u32[]{:S(2)}, u32[]{:S(2)}) async-start(f32[32,8,512]{2,1,0:T(8,128)} %broadcast_in_dim.28), calls=%async_computation.4 | async-start | bytes 1048576 | tf_op jit(solution)/shard_map/all_to_all | solution.py:236
  127.0 19.5 %collective-permute-start.1 = (f32[32,24,128]{2,1,0:T(8,128)S(1)}, f32[32,24,128]{2,1,0:T(8,128)}, u32[]{:S(2)}, u32[]{:S(2)}) collective-permute-start(f32[32,24,128]{2,1,0:T(8,128)S(1)} %all-to-all-done.2.mine_ref), channel_id=1, source_target_pairs={{0,8},{8,0},{1,9},{9,1},{2,10},{10,2},{3,11},{11,3},{4,12},{12,4},... | collective-permute-start | bytes 1179656 | tf_op jit(solution)/shard_map/ppermute | solution.py:267
  139.6 33.0 %collective-permute-start.10 = (f32[256,512]{1,0:T(8,128)}, f32[256,512]{1,0:T(8,128)}, u32[]{:S(2)}, u32[]{:S(2)}) collective-permute-start(f32[256,512]{1,0:T(8,128)} %bitcast.2), channel_id=1, source_target_pairs={{0,8},{8,0},{1,9},{9,1},{2,10},{10,2},{3,11},{11,3},{4,12},{12,4},... | collective-permute-start | bytes 1572872 | tf_op jit(solution)/shard_map/ppermute | solution.py:278
  170.3 2.3 %copy-start.2 = (f32[512,512]{1,0:T(8,128)S(1)}, f32[512,512]{1,0:T(8,128)}, u32[]{:S(2)}) copy-start(f32[512,512]{1,0:T(8,128)} %get-tuple-element.13) | copy-start | bytes 3145732

commit v4 on v3

--- a/solution.py
+++ b/solution.py
@@ -236,27 +236,35 @@
     return lax.all_to_all(copies, axes, 0, 0, tiled=True)
 
 
+def gather_block(panel):
+    depth, place, each = lax.axis_size("z"), lax.axis_index("z"), panel.shape[0]
+    pairs = depth // 2
+    odd, mine = place % 2, place // 2
+    swaps = ([(i, i ^ 1) for i in range(depth)], [(i, (i + (1 if i % 2 else -1)) % depth) for i in range(depth)])
+    other = lax.ppermute(panel, "z", swaps[0])
+    held = jnp.where(odd == 0, jnp.concatenate([panel, other]), jnp.concatenate([other, panel]))
+    block = jnp.zeros((depth * each, B), jnp.float32)
+    block = lax.dynamic_update_slice(block, held, (mine * 2 * each, 0))
+    step = 2 * odd - 1
+    for k in range(2, pairs + 1):
+        held = lax.ppermute(held, "z", swaps[(k + 1) % 2])
+        back = (k // 2) * (step if k % 2 == 0 else -step)
+        block = lax.dynamic_update_slice(block, held, ((mine + back + depth) % pairs * 2 * each, 0))
+    return block
+
+
 def per_device(panel, trailing):
     high = lax.Precision.HIGH
     plane = ("x", "y")
     ring, depth = lax.axis_size(plane), lax.axis_size("z")
     total_rows = panel.shape[0] * ring * depth * 2
     core = lax.axis_index("c")
-    place = lax.axis_index("z")
     swap = [(0, 1), (1, 0)]
     h = B // 2
     each = panel.shape[0]
     which = jnp.full((1,), core, jnp.int32)
 
-    block = jnp.zeros((depth * each, B), jnp.float32)
-    block = lax.dynamic_update_slice(block, panel, (place * each, 0))
-    forth = back = panel
-    for k in range(1, depth // 2 + 1):
-        forth = lax.ppermute(forth, "z", [(i, (i + 1) % depth) for i in range(depth)])
-        block = lax.dynamic_update_slice(block, forth, ((place + depth - k) % depth * each, 0))
-        if k < depth - k:
-            back = lax.ppermute(back, "z", [(i, (i - 1) % depth) for i in range(depth)])
-            block = lax.dynamic_update_slice(block, back, ((place + k) % depth * each, 0))
+    block = gather_block(panel)
 
     partner = lax.ppermute(panel, "c", swap)
     half = gram(which, panel, partner)

time: 179 us -> 179 us (level)
  starting transfers between devices: 86.3 us -> 82.6 us
  waiting for transfers between devices: 44.8 us -> 48.1 us
    ppermute x7 -> x4, waiting for transfers between devices: 8.02 us -> 15.8 us  [the longest x3 12.6 us: gather_block(): held = lax.ppermute(held, 'z', swaps[(k + 1) % 2])]
    ppermute x1, starting transfers between devices: 8.88 us -> 4.01 us  [per_device(): partner = lax.ppermute(panel, 'c', swap)]
    all_to_all x3, waiting for transfers between devices: 23.2 us -> 19.7 us  [spread(): return lax.all_to_all(copies, axes, 0, 0, tiled=True)]
    ppermute x7 -> x4, starting transfers between devices: 22.3 us -> 22.2 us  [the longest x3 17.2 us: gather_block(): held = lax.ppermute(held, 'z', swaps[(k + 1) % 2])]
  transfers between devices with their start and end apart: 16 -> 13, of which waited for: 7 -> 7; matrix products, arithmetic and copies ran while one was open for 7% -> 7% of each run, Pallas kernels for 15% -> 15%
where the time goes in v4:
time: 179 us; the launch traced here: 177 us
  starting transfers between devices  82.6 us (46%)
  waiting for transfers between devices  48.1 us (27%)
  Pallas kernels  26.4 us (15%)
  matrix products  9.54 us (5%)
  local copies, waits for them, and re-layouts  6.3 us (4%)
  other arithmetic  3.15 us (2%)
    all_to_all x3, waiting for transfers between devices, spread(): return lax.all_to_all(copies, axes, 0, 0, tiled=True)  19.7 us
    all_to_all x3, starting transfers between devices, spread(): return lax.all_to_all(copies, axes, 0, 0, tiled=True)  17.8 us
    ppermute x3, starting transfers between devices, gather_block(): held = lax.ppermute(held, 'z', swaps[(k + 1) % 2])  17.2 us
    ppermute x3, waiting for transfers between devices, gather_block(): held = lax.ppermute(held, 'z', swaps[(k + 1) % 2])  12.6 us
    all_to_all x1, waiting for transfers between devices, per_device(): lax.all_to_all((keep + got).reshape(ring, h // ring, -1), plane, 0, 0, ti...  12.5 us
    pallas_call x1, Pallas kernels, factor_low(): pl.pallas_call(low_kernel, out_shape=[jax.ShapeDtypeStruct((B, B), F32)]...  12.3 us
    pallas_call x1, Pallas kernels, factor_top(): pl.pallas_call(functools.partial(top_kernel, 1.0 / math.sqrt(total_rows))...  11.5 us
    all_to_all x1, starting transfers between devices, per_device(): pieces = lax.all_to_all(half.reshape(ring, -1, NB), plane, 0, 0, tiled=True)  9.8 us
  transfers between devices with their start and end apart: 13, of which 7 were waited for; matrix products, arithmetic and copies ran while one was open for 7% of the time, Pallas kernels for 15%

profile of v4, /device:TPU:1, one launch (start us, length us, event | category | flops | bytes accessed | tf_op | source)
XLA Modules:
  0.0 177.0 jit_solution(15281041441613027495)
XLA Ops:
  0.6 0.0 copy-start.3
  0.6 5.0 %collective-permute-start.2 = (f32[96,512]{1,0:T(8,128)}, f32[96,512]{1,0:T(8,128)S(1)}, u32[]{:S(2)}, u32[]{:S(2)}) collective-permute-start(f32[96,512]{1,0:T(8,128)} %a_ref.1), channel_id=1, source_target_pairs={{0,1},{1,0},{2,3},{3,2},{4,5},{5,4},{6,7},{7,6},{8,9},{9,8},{10,11... | collective-permute-start | bytes 589832 | tf_op jit(solution)/shard_map/ppermute | solution.py:244
  5.6 3.2 %collective-permute-done.2 = f32[96,512]{1,0:T(8,128)S(1)} collective-permute-done((f32[96,512]{1,0:T(8,128)}, f32[96,512]{1,0:T(8,128)S(1)}, u32[]{:S(2)}, u32[]{:S(2)}) %collective-permute-start.2) | collective-permute-done | bytes 196640 | tf_op jit(solution)/shard_map/ppermute | solution.py:244
  8.9 0.2 broadcast_in_dim.13
  9.0 0.0 copy-done.3
  9.1 0.1 constant_dynamic-update-slice_fusion.3
  9.2 11.3 %collective-permute-start.3 = (f32[192,512]{1,0:T(8,128)S(1)}, f32[192,512]{1,0:T(8,128)S(1)}, u32[]{:S(2)}, u32[]{:S(2)}) collective-permute-start(f32[192,512]{1,0:T(8,128)S(1)} %get-tuple-element.15), channel_id=1, source_target_pairs={{0,7},{1,2},{2,1},{3,4},{4,3},{5,6},{6,5},{7,0},{8,15},{9,10},{10,... | collective-permute-start | bytes 1179656 | tf_op jit(solution)/shard_map/ppermute | solution.py:250
  20.5 7.9 %collective-permute-done.3 = f32[192,512]{1,0:T(8,128)S(1)} collective-permute-done((f32[192,512]{1,0:T(8,128)S(1)}, f32[192,512]{1,0:T(8,128)S(1)}, u32[]{:S(2)}, u32[]{:S(2)}) %collective-permute-start.3) | collective-permute-done | bytes 393248 | tf_op jit(solution)/shard_map/ppermute | solution.py:250
  28.4 1.9 %collective-permute-start.4 = (f32[192,512]{1,0:T(8,128)S(1)}, f32[192,512]{1,0:T(8,128)}, u32[]{:S(2)}, u32[]{:S(2)}) collective-permute-start(f32[192,512]{1,0:T(8,128)S(1)} %collective-permute-done.3), channel_id=1, source_target_pairs={{0,1},{1,0},{2,3},{3,2},{4,5},{5,4},{6,7},{7,6},{8,9},{9,8},{10,11... | collective-permute-start | bytes 1179656 | tf_op jit(solution)/shard_map/ppermute | solution.py:250
  30.3 4.0 %collective-permute-start = (f32[96,512]{1,0:T(8,128)S(1)}, f32[96,512]{1,0:T(8,128)S(1)}, u32[]{:S(2)}, u32[]{:S(2)}) collective-permute-start(f32[96,512]{1,0:T(8,128)S(1)} %copy-done.3), channel_id=1, source_target_pairs={{0,8},{8,0},{1,9},{9,1},{2,10},{10,2},{3,11},{11,3},{4,12},{12,4},... | collective-permute-start | bytes 589832 | tf_op jit(solution)/shard_map/ppermute | solution.py:269
  34.4 4.6 %collective-permute-done.4 = f32[192,512]{1,0:T(8,128)} collective-permute-done((f32[192,512]{1,0:T(8,128)S(1)}, f32[192,512]{1,0:T(8,128)}, u32[]{:S(2)}, u32[]{:S(2)}) %collective-permute-start.4) | collective-permute-done | bytes 393248 | tf_op jit(solution)/shard_map/ppermute | solution.py:250
  39.0 4.0 %collective-permute-start.5 = (f32[192,512]{1,0:T(8,128)}, f32[192,512]{1,0:T(8,128)}, u32[]{:S(2)}, u32[]{:S(2)}) collective-permute-start(f32[192,512]{1,0:T(8,128)} %collective-permute-done.4), channel_id=1, source_target_pairs={{0,7},{1,2},{2,1},{3,4},{4,3},{5,6},{6,5},{7,0},{8,15},{9,10},{10,... | collective-permute-start | bytes 1179656 | tf_op jit(solution)/shard_map/ppermute | solution.py:250
  43.1 0.0 collective-permute-done.b_ref
  43.1 0.7 copy-done.5
  43.7 2.6 %gram.1 = f32[32,24,128]{2,1,0:T(8,128)} custom-call(s32[1]{0:T(128)} %bitcast.which, f32[96,512]{1,0:T(8,128)} %a_ref.1, f32[96,512]{1,0:T(8,128)} %copy-done.5), custom_call_target="tpu_custom_call" | custom-call | tf_op jit(solution)/shard_map/gram/pallas_call | solution.py:197
  46.4 9.8 %all-to-all-start = ((f32[32,24,128]{2,1,0:T(8,128)}), f32[32,24,128]{2,1,0:T(8,128)S(1)}, u32[]{:S(2)}, u32[]{:S(2)}) async-start(f32[32,24,128]{2,1,0:T(8,128)} %gram.1), calls=%async_computation | async-start | bytes 786432 | tf_op jit(solution)/shard_map/all_to_all | solution.py:271
  56.2 1.0 constant_dynamic-update-slice_fusion.2
  57.2 1.0 constant_dynamic-update-slice_fusion.1
  58.2 0.0 collective-permute-done.5
  58.2 1.0 constant_dynamic-update-slice_fusion
  59.3 0.0 copy-done
  59.3 1.6 fusion
  60.9 5.7 %collective-permute-start.6 = (f32[256,512]{1,0:T(8,128)}, f32[256,512]{1,0:T(8,128)}, u32[]{:S(2)}, u32[]{:S(2)}) collective-permute-start(f32[256,512]{1,0:T(8,128)} %fusion), channel_id=1, source_target_pairs={{0,8},{8,0},{1,9},{9,1},{2,10},{10,2},{3,11},{11,3},{4,12},{12,4},... | collective-permute-start | bytes 1572872 | tf_op jit(solution)/shard_map/ppermute | solution.py:280
  66.7 0.0 all-to-all-done
  66.7 0.6 broadcast_in_dim.11
  67.4 3.4 %all-to-all-start.1 = ((f32[8,24,128]{2,1,0:T(8,128)}), f32[8,24,128]{2,1,0:T(8,128)S(1)}, u32[]{:S(2)}, u32[]{:S(2)}) async-start(f32[8,24,128]{2,1,0:T(8,128)} %broadcast_in_dim.11), calls=%async_computation.1 | async-start | bytes 196608 | tf_op jit(solution)/shard_map/all_to_all | solution.py:236
  70.7 0.9 fusion.2
  71.7 0.0 collective-permute-done.6
  71.7 1.9 %add_bitcast_fusion = f32[32,8,512]{2,1,0:T(8,128)} fusion(f32[256,512]{1,0:T(8,128)S(1)} %fusion.2, f32[256,512]{1,0:T(8,128)} %collective-permute-done.6), kind=kLoop, calls=%fused_computation.7 | loop fusion | flops 131072 | bytes 1572864 | tf_op jit(solution)/shard_map/reshape | solution.py:283
  73.6 4.6 %all-to-all-done.1 = f32[8,24,128]{2,1,0:T(8,128)S(1)} async-done(((f32[8,24,128]{2,1,0:T(8,128)}), f32[8,24,128]{2,1,0:T(8,128)S(1)}, u32[]{:S(2)}, u32[]{:S(2)}) %all-to-all-start.1) | async-done | bytes 98336 | tf_op jit(solution)/shard_map/all_to_all | solution.py:236
  78.2 9.5 %all-to-all-start.3 = ((f32[32,8,512]{2,1,0:T(8,128)}), f32[32,8,512]{2,1,0:T(8,128)}, u32[]{:S(2)}, u32[]{:S(2)}) async-start(f32[32,8,512]{2,1,0:T(8,128)} %add_bitcast_fusion), calls=%async_computation.3 | async-start | bytes 1048576 | tf_op jit(solution)/shard_map/all_to_all | solution.py:283
  87.8 12.5 %all-to-all-done.3 = f32[32,8,512]{2,1,0:T(8,128)} async-done(((f32[32,8,512]{2,1,0:T(8,128)}), f32[32,8,512]{2,1,0:T(8,128)}, u32[]{:S(2)}, u32[]{:S(2)}) %all-to-all-start.3) | async-done | bytes 524320 | tf_op jit(solution)/shard_map/all_to_all | solution.py:283
  100.3 0.8 broadcast_in_dim.12
  101.1 7.7 %all-to-all-start.2 = ((f32[32,24,128]{2,1,0:T(8,128)}), f32[32,24,128]{2,1,0:T(8,128)S(1)}, u32[]{:S(2)}, u32[]{:S(2)}) async-start(f32[32,24,128]{2,1,0:T(8,128)} %broadcast_in_dim.12), calls=%async_computation.2 | async-start | bytes 786432 | tf_op jit(solution)/shard_map/all_to_all | solution.py:236
  108.8 1.1 reduce_sum.29
  109.9 9.2 %all-to-all-done.2.mine_ref = f32[32,24,128]{2,1,0:T(8,128)S(1)} async-done(((f32[32,24,128]{2,1,0:T(8,128)}), f32[32,24,128]{2,1,0:T(8,128)S(1)}, u32[]{:S(2)}, u32[]{:S(2)}) %all-to-all-start.2) | async-done | bytes 393248 | tf_op jit(solution)/shard_map/all_to_all | solution.py:236
  119.1 0.9 broadcast_in_dim.28
  120.0 6.7 %all-to-all-start.4 = ((f32[32,8,512]{2,1,0:T(8,128)}), f32[32,8,512]{2,1,0:T(8,128)}, u32[]{:S(2)}, u32[]{:S(2)}) async-start(f32[32,8,512]{2,1,0:T(8,128)} %broadcast_in_dim.28), calls=%async_computation.4 | async-start | bytes 1048576 | tf_op jit(solution)/shard_map/all_to_all | solution.py:236
  126.7 5.7 %collective-permute-start.1 = (f32[32,24,128]{2,1,0:T(8,128)S(1)}, f32[32,24,128]{2,1,0:T(8,128)}, u32[]{:S(2)}, u32[]{:S(2)}) collective-permute-start(f32[32,24,128]{2,1,0:T(8,128)S(1)} %all-to-all-done.2.mine_ref), channel_id=1, source_target_pairs={{0,8},{8,0},{1,9},{9,1},{2,10},{10,2},{3,11},{11,3},{4,12},{12,4},... | collective-permute-start | bytes 1179656 | tf_op jit(solution)/shard_map/ppermute | solution.py:275
  132.4 5.9 %all-to-all-done.4 = f32[32,8,512]{2,1,0:T(8,128)} async-done(((f32[32,8,512]{2,1,0:T(8,128)}), f32[32,8,512]{2,1,0:T(8,128)}, u32[]{:S(2)}, u32[]{:S(2)}) %all-to-all-start.4) | async-done | bytes 524320 | tf_op jit(solution)/shard_map/all_to_all | solution.py:236
  138.4 7.9 %collective-permute-start.7 = (f32[256,512]{1,0:T(8,128)}, f32[256,512]{1,0:T(8,128)}, u32[]{:S(2)}, u32[]{:S(2)}) collective-permute-start(f32[256,512]{1,0:T(8,128)} %bitcast.2), channel_id=1, source_target_pairs={{0,8},{8,0},{1,9},{9,1},{2,10},{10,2},{3,11},{11,3},{4,12},{12,4},... | collective-permute-start | bytes 1572872 | tf_op jit(solution)/shard_map/ppermute | solution.py:286
  146.2 0.0 collective-permute-done.1.other_ref
  146.3 11.5 %factor_top.1 = (f32[256,512]{1,0:T(8,128)}, f32[256,256]{1,0:T(8,128)}, f32[256,512]{1,0:T(8,128)}, f32[8,512]{1,0:T(8,128)}) custom-call(s32[1]{0:T(128)} %bitcast.which, f32[32,24,128]{2,1,0:T(8,128)} %copy-done.1, f32[32,24,128]{2,1,0:T(8,128)} %collective-permute-done.1.other_ref), custom_call_target="tpu_custom_call" | custom-call | tf_op jit(solution)/shard_map/factor_top/pallas_call | solution.py:208
  157.7 12.3 %factor_low.1 = (f32[512,512]{1,0:T(8,128)}, f32[512,512]{1,0:T(8,128)}) custom-call(s32[1]{0:T(128)} %bitcast.which, f32[256,512]{1,0:T(8,128)} %get-tuple-element.8.top_ref, f32[256,256]{1,0:T(8,128)} %get-tuple-element.9.mtop_ref, f32[256,512]{1,0:T(8,128)} %get-tuple-element.10.tail_ref, f32[8,512]{1,0:T(8,128)} %get-tuple-element.11.s_ref), custom_call_target="tpu_custom_call" | custom-call | tf_op jit(solution)/shard_map/factor_low/pallas_call | solution.py:220
  170.0 2.3 %fusion.5 = f32[512,512]{1,0:T(8,128)S(1)} fusion(f32[512,512]{1,0:T(8,128)} %get-tuple-element.13, f32[32,8,512]{2,1,0:T(8,128)} %all-to-all-done.4), kind=kOutput, calls=%fused_computation.8 | convolution fusion | flops 805306368 | bytes 2097152 | tf_op jit(solution)/shard_map/dot_general | solution.py:231
  172.3 0.0 collective-permute-done.7
  172.3 2.1 %convolution_add_fusion = f32[512,512]{1,0:T(8,128)S(1)} fusion(f32[512,512]{1,0:T(8,128)S(1)} %fusion.5, f32[256,512]{1,0:T(8,128)} %collective-permute-done.7, f32[512,512]{1,0:T(8,128)S(1)} %copy-done.2), kind=kOutput, calls=%fused_computation.1 | convolution fusion | flops 805568512 | bytes 3145728 | tf_op jit(solution)/shard_map/dot_general | solution.py:231
  174.5 2.6 %convolution_subtract_fusion = f32[768,512]{1,0:T(8,128)} fusion(f32[768,512]{1,0:T(8,128)S(1)} %copy-done, f32[768,512]{1,0:T(8,128)S(1)} %constant_dynamic-update-slice_fusion, f32[512,512]{1,0:T(8,128)S(1)} %convolution_add_fusion), kind=kOutput, calls=%fused_computation | convolution fusion | flops 1208352768 | bytes 5767168 | tf_op jit(solution)/shard_map/dot_general | solution.py:231
  (10 shorter events, 0.1 us)
Async XLA Ops:
  0.6 8.4 %copy-start.3 = (f32[96,512]{1,0:T(8,128)S(1)}, f32[96,512]{1,0:T(8,128)}, u32[]{:S(2)}) copy-start(f32[96,512]{1,0:T(8,128)} %a_ref.1) | copy-start | bytes 589828
  0.6 8.2 %collective-permute-start.2 = (f32[96,512]{1,0:T(8,128)}, f32[96,512]{1,0:T(8,128)S(1)}, u32[]{:S(2)}, u32[]{:S(2)}) collective-permute-start(f32[96,512]{1,0:T(8,128)} %a_ref.1), channel_id=1, source_target_pairs={{0,1},{1,0},{2,3},{3,2},{4,5},{5,4},{6,7},{7,6},{8,9},{9,8},{10,11... | collective-permute-start | bytes 589832 | tf_op jit(solution)/shard_map/ppermute | solution.py:244
  9.2 19.3 %collective-permute-start.3 = (f32[192,512]{1,0:T(8,128)S(1)}, f32[192,512]{1,0:T(8,128)S(1)}, u32[]{:S(2)}, u32[]{:S(2)}) collective-permute-start(f32[192,512]{1,0:T(8,128)S(1)} %get-tuple-element.15), channel_id=1, source_target_pairs={{0,7},{1,2},{2,1},{3,4},{4,3},{5,6},{6,5},{7,0},{8,15},{9,10},{10,... | collective-permute-start | bytes 1179656 | tf_op jit(solution)/shard_map/ppermute | solution.py:250
  28.4 5.9 %copy-start.4 = (f32[192,512]{1,0:T(8,128)}, f32[192,512]{1,0:T(8,128)S(1)}, u32[]{:S(2)}) copy-start(f32[192,512]{1,0:T(8,128)S(1)} %collective-permute-done.3) | copy-start | bytes 1179652
  28.4 10.6 %collective-permute-start.4 = (f32[192,512]{1,0:T(8,128)S(1)}, f32[192,512]{1,0:T(8,128)}, u32[]{:S(2)}, u32[]{:S(2)}) collective-permute-start(f32[192,512]{1,0:T(8,128)S(1)} %collective-permute-done.3), channel_id=1, source_target_pairs={{0,1},{1,0},{2,3},{3,2},{4,5},{5,4},{6,7},{7,6},{8,9},{9,8},{10,11... | collective-permute-start | bytes 1179656 | tf_op jit(solution)/shard_map/ppermute | solution.py:250
  30.3 12.7 %collective-permute-start = (f32[96,512]{1,0:T(8,128)S(1)}, f32[96,512]{1,0:T(8,128)S(1)}, u32[]{:S(2)}, u32[]{:S(2)}) collective-permute-start(f32[96,512]{1,0:T(8,128)S(1)} %copy-done.3), channel_id=1, source_target_pairs={{0,8},{8,0},{1,9},{9,1},{2,10},{10,2},{3,11},{11,3},{4,12},{12,4},... | collective-permute-start | bytes 589832 | tf_op jit(solution)/shard_map/ppermute | solution.py:269
  39.0 19.3 %collective-permute-start.5 = (f32[192,512]{1,0:T(8,128)}, f32[192,512]{1,0:T(8,128)}, u32[]{:S(2)}, u32[]{:S(2)}) collective-permute-start(f32[192,512]{1,0:T(8,128)} %collective-permute-done.4), channel_id=1, source_target_pairs={{0,7},{1,2},{2,1},{3,4},{4,3},{5,6},{6,5},{7,0},{8,15},{9,10},{10,... | collective-permute-start | bytes 1179656 | tf_op jit(solution)/shard_map/ppermute | solution.py:250
  43.1 0.7 copy-start.5
  46.4 12.9 %copy-start = (f32[768,512]{1,0:T(8,128)S(1)}, f32[768,512]{1,0:T(8,128)}, u32[]{:S(2)}) copy-start(f32[768,512]{1,0:T(8,128)} %param.3) | copy-start | bytes 4718596
  46.4 20.3 %all-to-all-start = ((f32[32,24,128]{2,1,0:T(8,128)}), f32[32,24,128]{2,1,0:T(8,128)S(1)}, u32[]{:S(2)}, u32[]{:S(2)}) async-start(f32[32,24,128]{2,1,0:T(8,128)} %gram.1), calls=%async_computation | async-start | bytes 786432 | tf_op jit(solution)/shard_map/all_to_all | solution.py:271
  60.9 10.7 %collective-permute-start.6 = (f32[256,512]{1,0:T(8,128)}, f32[256,512]{1,0:T(8,128)}, u32[]{:S(2)}, u32[]{:S(2)}) collective-permute-start(f32[256,512]{1,0:T(8,128)} %fusion), channel_id=1, source_target_pairs={{0,8},{8,0},{1,9},{9,1},{2,10},{10,2},{3,11},{11,3},{4,12},{12,4},... | collective-permute-start | bytes 1572872 | tf_op jit(solution)/shard_map/ppermute | solution.py:280
  67.4 10.9 %all-to-all-start.1 = ((f32[8,24,128]{2,1,0:T(8,128)}), f32[8,24,128]{2,1,0:T(8,128)S(1)}, u32[]{:S(2)}, u32[]{:S(2)}) async-start(f32[8,24,128]{2,1,0:T(8,128)} %broadcast_in_dim.11), calls=%async_computation.1 | async-start | bytes 196608 | tf_op jit(solution)/shard_map/all_to_all | solution.py:236
  78.2 22.1 %all-to-all-start.3 = ((f32[32,8,512]{2,1,0:T(8,128)}), f32[32,8,512]{2,1,0:T(8,128)}, u32[]{:S(2)}, u32[]{:S(2)}) async-start(f32[32,8,512]{2,1,0:T(8,128)} %add_bitcast_fusion), calls=%async_computation.3 | async-start | bytes 1048576 | tf_op jit(solution)/shard_map/all_to_all | solution.py:283
  101.1 18.0 %all-to-all-start.2 = ((f32[32,24,128]{2,1,0:T(8,128)}), f32[32,24,128]{2,1,0:T(8,128)S(1)}, u32[]{:S(2)}, u32[]{:S(2)}) async-start(f32[32,24,128]{2,1,0:T(8,128)} %broadcast_in_dim.12), calls=%async_computation.2 | async-start | bytes 786432 | tf_op jit(solution)/shard_map/all_to_all | solution.py:236
  119.1 27.2 %copy-start.1 = (f32[32,24,128]{2,1,0:T(8,128)}, f32[32,24,128]{2,1,0:T(8,128)S(1)}, u32[]{:S(2)}) copy-start(f32[32,24,128]{2,1,0:T(8,128)S(1)} %all-to-all-done.2.mine_ref) | copy-start | bytes 1179652
  120.0 18.4 %all-to-all-start.4 = ((f32[32,8,512]{2,1,0:T(8,128)}), f32[32,8,512]{2,1,0:T(8,128)}, u32[]{:S(2)}, u32[]{:S(2)}) async-start(f32[32,8,512]{2,1,0:T(8,128)} %broadcast_in_dim.28), calls=%async_computation.4 | async-start | bytes 1048576 | tf_op jit(solution)/shard_map/all_to_all | solution.py:236
  126.7 19.6 %collective-permute-start.1 = (f32[32,24,128]{2,1,0:T(8,128)S(1)}, f32[32,24,128]{2,1,0:T(8,128)}, u32[]{:S(2)}, u32[]{:S(2)}) collective-permute-start(f32[32,24,128]{2,1,0:T(8,128)S(1)} %all-to-all-done.2.mine_ref), channel_id=1, source_target_pairs={{0,8},{8,0},{1,9},{9,1},{2,10},{10,2},{3,11},{11,3},{4,12},{12,4},... | collective-permute-start | bytes 1179656 | tf_op jit(solution)/shard_map/ppermute | solution.py:275
  138.4 34.0 %collective-permute-start.7 = (f32[256,512]{1,0:T(8,128)}, f32[256,512]{1,0:T(8,128)}, u32[]{:S(2)}, u32[]{:S(2)}) collective-permute-start(f32[256,512]{1,0:T(8,128)} %bitcast.2), channel_id=1, source_target_pairs={{0,8},{8,0},{1,9},{9,1},{2,10},{10,2},{3,11},{11,3},{4,12},{12,4},... | collective-permute-start | bytes 1572872 | tf_op jit(solution)/shard_map/ppermute | solution.py:286
  170.0 2.3 %copy-start.2 = (f32[512,512]{1,0:T(8,128)S(1)}, f32[512,512]{1,0:T(8,128)}, u32[]{:S(2)}) copy-start(f32[512,512]{1,0:T(8,128)} %get-tuple-element.13) | copy-start | bytes 3145732
